TPU v7x, 32 devices: a whole 2x2x4 slice. The times are simulated.
32 devices in a mesh: real: 4 (over z), rows: 4 (over y, core), field: 2 (over x).
Axes of the slice: x: 2, y: 2, z: 4, core: 2. Of those that a mesh axis runs over, the one named last changes fastest.
Arguments:
- sims: bfloat16 [4, 2, 2048, 2048], P('real', 'field', 'rows'), may hold values from -6 to 6
- data: bfloat16 [2, 2048, 2048], P('field', 'rows'), may hold values from -6 to 6
- mask_flags: int32 [16, 16], P('rows'), may hold values 0 or 1
- bins: int32 [512, 512], P(None, 'rows'), may hold values from 0 to 63
- cl_signal: float32 [2, 64], P('field'), may hold values from 0.5 to 4
- cl_noise: float32 [2, 64], P('field'), may hold values from 0.1 to 2
- norm: float32 [64], replicated, may hold values from 0.5 to 2
- matching: int32 [4], replicated, may hold values from 0 to 3, each once
Outputs:
- estimates: float32 [4, 2, 2, 512, 512], P('real', None, None, None, 'rows')
Inputs may be any that keep to these rules, and one draw needn't show every extreme that they name: `matching`: each realization index appears exactly once.
All inputs are finite; a program needn't handle non-finite values. No bound on the sum of `mask_flags` on one device may be relied on, other than what follows from the above.
Results may differ from a plain program's by a relative error of at most 0.011.
Values may be sent and summed in bfloat16 or wider, within the bound.
A program may use at most 128 MiB of HBM per device.

v0:
```python
import math

import jax
import jax.numpy as jnp
from jax import lax
from jax.sharding import PartitionSpec as P

TILE = 128


def tables(npix, kf, scale):
    pixel = jnp.arange(npix, dtype=jnp.int32)
    freq = jnp.arange(kf, dtype=jnp.int32) - kf // 2
    phase = jnp.mod(pixel[:, None] * freq[None, :], npix)
    angle = phase.astype(jnp.float32) * (2.0 * math.pi / npix)
    return (
        (jnp.cos(angle) * scale).astype(jnp.bfloat16),
        (jnp.sin(angle) * scale).astype(jnp.bfloat16),
    )


def expand_mask(flags, tile):
    first, second = flags.shape
    full = jnp.broadcast_to(flags[:, None, :, None], (first, tile, second, tile))
    return full.reshape(first * tile, second * tile) > 0


def column_part(maps, cos_t, sin_t):
    count, height, width = maps.shape
    flat = maps.reshape(count * height, width)
    a_re = (
        jnp.dot(flat, cos_t, preferred_element_type=jnp.float32)
        .astype(jnp.bfloat16)
        .reshape(count, height, -1)
    )
    a_im = (
        (-jnp.dot(flat, sin_t, preferred_element_type=jnp.float32))
        .astype(jnp.bfloat16)
        .reshape(count, height, -1)
    )
    return (a_re, a_im)


def row_part(a_re, a_im, cos_t, sin_t):
    a_re, a_im = (
        lax.all_to_all(a_re, "rows", split_axis=2, concat_axis=1, tiled=True),
        lax.all_to_all(a_im, "rows", split_axis=2, concat_axis=1, tiled=True),
    )
    x_re = jnp.einsum("yk,myj->mkj", cos_t, a_re, preferred_element_type=jnp.float32) + jnp.einsum(
        "yk,myj->mkj", sin_t, a_im, preferred_element_type=jnp.float32
    )
    x_im = jnp.einsum("yk,myj->mkj", cos_t, a_im, preferred_element_type=jnp.float32) - jnp.einsum(
        "yk,myj->mkj", sin_t, a_re, preferred_element_type=jnp.float32
    )
    return (x_re, x_im)


def inverse(z_re, z_im, icos, isin):
    count = z_re.shape[0]
    y_re = (
        jnp.einsum("yk,mkj->myj", icos, z_re, preferred_element_type=jnp.float32)
        - jnp.einsum("yk,mkj->myj", isin, z_im, preferred_element_type=jnp.float32)
    ).astype(jnp.bfloat16)
    y_im = (
        jnp.einsum("yk,mkj->myj", icos, z_im, preferred_element_type=jnp.float32)
        + jnp.einsum("yk,mkj->myj", isin, z_re, preferred_element_type=jnp.float32)
    ).astype(jnp.bfloat16)
    y_re, y_im = (
        lax.all_to_all(y_re, "rows", split_axis=1, concat_axis=2, tiled=True),
        lax.all_to_all(y_im, "rows", split_axis=1, concat_axis=2, tiled=True),
    )
    height = y_re.shape[1]
    flat_re = y_re.reshape(count * height, -1)
    flat_im = y_im.reshape(count * height, -1)
    out = jnp.dot(flat_re, icos.T, preferred_element_type=jnp.float32) - jnp.dot(
        flat_im, isin.T, preferred_element_type=jnp.float32
    )
    return out.astype(jnp.bfloat16).reshape(count, height, -1)


def filter_legs(x_re, x_im, wcell, gcell, lx, ly):
    grad_x = lx * gcell
    grad_y = ly * gcell
    z_re = jnp.stack([wcell * x_re, -grad_x * x_im, -grad_y * x_im])
    z_im = jnp.stack([wcell * x_im, grad_x * x_re, grad_y * x_re])
    return (z_re.astype(jnp.bfloat16), z_im.astype(jnp.bfloat16))


def select_rows(piece, partner_id):
    count = piece.shape[0]
    hit = jnp.arange(count, dtype=jnp.int32) == partner_id
    hit = hit.reshape((count,) + (1,) * (piece.ndim - 1))
    return jnp.sum(jnp.where(hit, piece, jnp.zeros_like(piece)), axis=0).astype(piece.dtype)


def lookup_cells(bins, values):
    nbins = values.shape[0]
    match_bin = bins[:, :, None] == jnp.arange(nbins, dtype=jnp.int32)[None, None, :]
    return jnp.sum(jnp.where(match_bin, values[None, None, :], jnp.zeros((), jnp.float32)), axis=2)


def body(sims, data, mask_flags, bins, cl_signal, cl_noise, norm, matching):
    npix = sims.shape[3]
    kf = bins.shape[0]
    cols = bins.shape[1]
    mask = expand_mask(mask_flags, TILE)
    stacked = jnp.concatenate([sims[0], data], axis=0)
    masked = jnp.where(mask[None], stacked, jnp.zeros_like(stacked))
    cos_t, sin_t = tables(npix, kf, npix ** (-0.5))
    icos, isin = tables(npix, kf, kf ** (-0.5))
    step_size = 2.0 * math.pi / npix
    col_freq = (lax.axis_index("rows") * cols + jnp.arange(cols, dtype=jnp.int32) - kf // 2).astype(
        jnp.float32
    ) * step_size
    row_freq = (jnp.arange(kf, dtype=jnp.int32) - kf // 2).astype(jnp.float32) * step_size
    lx = jnp.broadcast_to(col_freq[None, :], (kf, cols))
    ly = jnp.broadcast_to(row_freq[:, None], (kf, cols))
    weight_vals = 1.0 / (cl_signal[0] + cl_noise[0])
    grad_vals = cl_signal[0] * weight_vals
    wcell = lookup_cells(bins, weight_vals)
    gcell = lookup_cells(bins, grad_vals)
    ncell = lookup_cells(bins, norm)
    first_re, first_im = column_part(masked, cos_t, sin_t)
    x_re, x_im = row_part(first_re, first_im, cos_t, sin_t)
    own_re, own_im = filter_legs(x_re[0], x_im[0], wcell, gcell, lx, ly)
    dat_re, dat_im = filter_legs(x_re[1], x_im[1], wcell, gcell, lx, ly)
    legs = inverse(
        jnp.concatenate([own_re, dat_re], axis=0),
        jnp.concatenate([own_im, dat_im], axis=0),
        icos,
        isin,
    )
    sim_legs = legs[0:3]
    data_legs = legs[3:6].astype(jnp.float32)
    real_index = lax.axis_index("real")
    partner_id = jnp.sum(
        jnp.where(jnp.arange(matching.shape[0], dtype=jnp.int32) == real_index, matching, 0)
    )
    empty = jnp.zeros_like(x_re[0])
    p_re = empty + select_rows(
        lax.all_gather(x_re[0:1].astype(jnp.bfloat16), "real", axis=0, tiled=True).astype(
            jnp.float32
        ),
        partner_id,
    )
    p_im = empty + select_rows(
        lax.all_gather(x_im[0:1].astype(jnp.bfloat16), "real", axis=0, tiled=True).astype(
            jnp.float32
        ),
        partner_id,
    )
    z_re, z_im = filter_legs(p_re, p_im, wcell, gcell, lx, ly)
    partner_legs = inverse(z_re, z_im, icos, isin)
    own = sim_legs.astype(jnp.float32)
    other = partner_legs.astype(jnp.float32)
    ds_x = data_legs[1] * own[0] + own[1] * data_legs[0]
    ss_x = own[1] * other[0] + other[1] * own[0]
    ds_y = data_legs[2] * own[0] + own[2] * data_legs[0]
    ss_y = own[2] * other[0] + other[2] * own[0]
    products = jnp.stack([ds_x, ss_x, ds_y, ss_y]).astype(jnp.bfloat16)
    height = products.shape[1]
    mine = lax.all_to_all(products[None], "field", split_axis=1, concat_axis=0, tiled=True)
    sources = mine.shape[0]
    part_re, part_im = column_part(mine.reshape(sources * 2, height, npix), cos_t, sin_t)
    sum_re = jnp.sum(part_re.astype(jnp.float32).reshape(sources, 2, height, -1), axis=0)
    sum_im = jnp.sum(part_im.astype(jnp.float32).reshape(sources, 2, height, -1), axis=0)
    s_re, s_im = row_part(sum_re.astype(jnp.bfloat16), sum_im.astype(jnp.bfloat16), cos_t, sin_t)
    direction = jnp.where(lax.axis_index("field") == 0, lx, ly)
    scale = ncell * direction
    terms = jnp.stack([-scale * s_im, scale * s_re], axis=1)
    total = lax.psum(terms.astype(jnp.bfloat16), "field").astype(jnp.float32)
    return total[None]


def solution(mesh):
    in_specs = (
        P("real", "field", "rows", None),
        P("field", "rows", None),
        P("rows", None),
        P(None, "rows"),
        P("field", None),
        P("field", None),
        P(),
        P(),
    )
    out_specs = P("real", None, None, None, "rows")
    return jax.shard_map(body, mesh=mesh, in_specs=in_specs, out_specs=out_specs, check_vma=False)
```

profile of v0, /device:TPU:0, one launch (start us, length us, event | category | flops | bytes accessed | tf_op | source)
XLA Modules:
  0.0 774.8 jit_solution(14107730076439929142)
XLA Ops:
  8.4 2.2 maximum_select_fusion
  10.6 16.8 %negate_convert_fusion.1 = bf16[1024,512]{1,0:T(8,128)(2,1)S(1)} fusion(bf16[1024,2048]{1,0:T(8,128)(2,1)S(1)} %bitcast.283, s32[512]{0:T(512)S(1)} %iota_add_fusion), kind=kOutput, calls=%fused_computation.84 | convolution fusion | flops 2165309440 | bytes 5244928 | tf_op jit(solution)/shard_map/dot_general | solution.py:37
  27.4 2.1 copy.71
  29.5 4.4 all-to-all-start.1
  34.0 18.9 %fusion.65 = bf16[1024,512]{1,0:T(8,128)(2,1)S(1)} fusion(bf16[1024,2048]{1,0:T(8,128)(2,1)} %bitcast.284, s32[512]{0:T(512)S(1)} %iota_add_fusion), kind=kOutput, calls=%fused_computation.94 | convolution fusion | flops 2164785152 | bytes 5244928 | tf_op jit(solution)/shard_map/dot_general | solution.py:32
  52.9 2.1 copy.69
  55.7 16.3 %select_reduce_fusion.2 = (f32[512,128]{1,0:T(8,128)}, f32[512,128]{1,0:T(8,128)S(1)}, f32[512,128]{1,0:T(8,128)S(1)}) fusion(f32[64]{0:T(128)S(1)} %copy-done.12, s32[512,128]{1,0:T(8,128)S(1)} %copy-done.7, f32[64]{0:T(128)S(1)} %get-tuple-element.12, f32[64]{0:T(128)S(1)} %get-tuple-element.13), kind=kLoop, calls=%fused_computation.3 | loop fusion | flops 29163520 | bytes 1049344 | tf_op jit(solution)/shard_map/reduce_sum | solution.py:99
  72.0 3.7 all-to-all-start
  76.7 1.8 copy.122
  78.5 1.8 all_to_all.110
  80.3 16.7 %fusion.46 = f32[2,128,512]{2,1,0:T(8,128)} fusion(bf16[2,2048,128]{1,2,0:T(8,128)(2,1)S(1)} %all_to_all.110, s32[512]{0:T(512)S(1)} %iota_add_fusion), kind=kOutput, calls=%fused_computation.74 | convolution fusion | flops 553648128 | bytes 1574912 | tf_op jit(solution)/shard_map/yk,myj->mkj/dot_general | solution.py:49
  98.6 1.0 copy-done.6
  99.6 16.5 %fusion.44 = f32[2,128,512]{2,1,0:T(8,128)S(1)} fusion(bf16[2,2048,128]{1,2,0:T(8,128)(2,1)S(1)} %all_to_all.106, s32[512]{0:T(512)S(1)} %iota_add_fusion), kind=kOutput, calls=%fused_computation.72 | convolution fusion | flops 553648128 | bytes 1574912 | tf_op jit(solution)/shard_map/yk,myj->mkj/dot_general | solution.py:52
  116.1 17.2 %fusion.69 = f32[2,512,128]{1,2,0:T(8,128)S(1)} fusion(f32[2,128,512]{2,1,0:T(8,128)S(1)} %copy-done.16, bf16[2,2048,128]{1,2,0:T(8,128)(2,1)} %copy-done.6, s32[512]{0:T(512)S(1)} %iota_add_fusion), kind=kOutput, calls=%fused_computation.96 | convolution fusion | flops 553779200 | bytes 2099200 | tf_op jit(solution)/shard_map/yk,myj->mkj/dot_general | solution.py:49
  133.4 15.9 %fusion.75 = f32[2,512,128]{1,2,0:T(8,128)S(1)} fusion(f32[2,128,512]{2,1,0:T(8,128)S(1)} %fusion.44, bf16[2,2048,128]{1,2,0:T(8,128)(2,1)S(1)} %copy-done.5, s32[512]{0:T(512)S(1)} %iota_add_fusion), kind=kOutput, calls=%fused_computation.98 | convolution fusion | flops 553779200 | bytes 2099200 | tf_op jit(solution)/shard_map/yk,myj->mkj/dot_general | solution.py:52
  149.6 0.9 copy-done.8
  150.5 0.9 copy-done.10
  151.5 17.2 %all_gather.6 = bf16[4,512,128]{2,1,0:T(8,128)(2,1)S(1)} all-gather(bf16[1,512,128]{2,1,0:T(8,128)(2,1)S(1)} %copy.78), channel_id=1, replica_groups=mesh['real'=4,'rows'=4,'field'=2] {'real'}, dimensions={0}, use_global_device_ids=true | all-gather | bytes 655360 | tf_op jit(solution)/shard_map/all_gather | solution.py:141
  168.8 15.6 %all_gather.7 = bf16[4,512,128]{2,1,0:T(8,128)(2,1)S(1)} all-gather(bf16[1,512,128]{2,1,0:T(8,128)(2,1)S(1)} %copy.80), channel_id=1, replica_groups=mesh['real'=4,'rows'=4,'field'=2] {'real'}, dimensions={0}, use_global_device_ids=true | all-gather | bytes 655360 | tf_op jit(solution)/shard_map/all_gather | solution.py:147
  185.2 16.0 %fusion.34 = f32[3,128,2048]{2,1,0:T(8,128)S(1)} fusion(s32[512]{0:T(512)S(1)} %iota_add_fusion, bf16[1,512,128]{1,2,0:T(8,128)(2,1)S(1)} %get-tuple-element.25, bf16[1,512,128]{1,2,0:T(8,128)(2,1)S(1)} %get-tuple-element.24, bf16[1,512,128]{1,2,0:T(8,128)(2,1)S(1)} %get-tuple-element.36), kind=kOutput, calls=%fused_computation.62 | convolution fusion | flops 822476800 | bytes 3540992 | tf_op jit(solution)/shard_map/yk,mkj->myj/dot_general | solution.py:61
  201.2 17.3 %fusion.32 = f32[3,128,2048]{2,1,0:T(8,128)} fusion(s32[512]{0:T(512)S(1)} %iota_add_fusion, bf16[1,512,128]{1,2,0:T(8,128)(2,1)S(1)} %get-tuple-element.34, bf16[1,512,128]{1,2,0:T(8,128)(2,1)S(1)} %get-tuple-element.35, bf16[1,512,128]{1,2,0:T(8,128)(2,1)S(1)} %get-tuple-element.37), kind=kOutput, calls=%fused_computation.60 | convolution fusion | flops 822476800 | bytes 3540992 | tf_op jit(solution)/shard_map/yk,mkj->myj/dot_general | solution.py:65
  218.5 16.7 %fusion.22 = bf16[3,2048,128]{1,2,0:T(8,128)(2,1)S(1)} fusion(f32[3,128,2048]{2,1,0:T(8,128)S(1)} %fusion.34, s32[512]{0:T(512)S(1)} %iota_add_fusion, bf16[1,512,128]{1,2,0:T(8,128)(2,1)S(1)} %get-tuple-element.34, bf16[1,512,128]{1,2,0:T(8,128)(2,1)S(1)} %get-tuple-element.35, bf16[1,512,128]{1,2,0:T(8,128)(2,1)S(1)} %get-tuple-element.37), kind=kOutput, calls=%fused_computation.50 | convolution fusion | flops 824049664 | bytes 5113856 | tf_op jit(solution)/shard_map/yk,mkj->myj/dot_general | solution.py:62
  235.2 2.6 copy.82
  237.8 3.8 all-to-all-start.4
  241.6 18.6 %fusion.23 = bf16[3,2048,128]{1,2,0:T(8,128)(2,1)} fusion(f32[3,128,2048]{2,1,0:T(8,128)} %fusion.32, s32[512]{0:T(512)S(1)} %iota_add_fusion, bf16[1,512,128]{1,2,0:T(8,128)(2,1)S(1)} %get-tuple-element.25, bf16[1,512,128]{1,2,0:T(8,128)(2,1)S(1)} %get-tuple-element.24, bf16[1,512,128]{1,2,0:T(8,128)(2,1)S(1)} %get-tuple-element.36), kind=kOutput, calls=%fused_computation.51 | convolution fusion | flops 824049664 | bytes 5113856 | tf_op jit(solution)/shard_map/yk,mkj->myj/dot_general | solution.py:66
  260.1 4.2 copy.84
  264.3 1.7 fusion.123
  266.0 1.7 fusion.126
  267.7 20.1 %fusion.38 = f32[6,128,2048]{2,1,0:T(8,128)} fusion(bf16[6,512,128]{1,2,0:T(8,128)(2,1)} %get-tuple-element.33, s32[512]{0:T(512)S(1)} %iota_add_fusion), kind=kOutput, calls=%fused_computation.66 | convolution fusion | flops 1627389952 | bytes 7079936 | tf_op jit(solution)/shard_map/yk,mkj->myj/dot_general | solution.py:61
  287.9 4.5 all-to-all-start.5
  293.8 20.4 %fusion.20 = bf16[6,2048,128]{1,2,0:T(8,128)(2,1)} fusion(f32[6,128,2048]{2,1,0:T(8,128)} %fusion.38, bf16[6,512,128]{1,2,0:T(8,128)(2,1)} %fusion.125, s32[512]{0:T(512)S(1)} %iota_add_fusion), kind=kOutput, calls=%fused_computation.47 | convolution fusion | flops 1630535680 | bytes 10225664 | tf_op jit(solution)/shard_map/yk,mkj->myj/dot_general | solution.py:62
  314.2 6.3 copy.74
  320.6 5.2 all-to-all-start.2
  325.8 16.4 %fusion.36 = f32[6,128,2048]{2,1,0:T(8,128)S(1)} fusion(bf16[6,512,128]{1,2,0:T(8,128)(2,1)S(1)} %copy-done.9, s32[512]{0:T(512)S(1)} %iota_add_fusion), kind=kOutput, calls=%fused_computation.64 | convolution fusion | flops 1627389952 | bytes 7079936 | tf_op jit(solution)/shard_map/yk,mkj->myj/dot_general | solution.py:65
  342.3 22.0 %fusion.21 = bf16[6,2048,128]{1,2,0:T(8,128)(2,1)} fusion(f32[6,128,2048]{2,1,0:T(8,128)S(1)} %fusion.36, bf16[6,512,128]{1,2,0:T(8,128)(2,1)S(1)} %copy-done.11, s32[512]{0:T(512)S(1)} %iota_add_fusion), kind=kOutput, calls=%fused_computation.48 | convolution fusion | flops 1630535680 | bytes 10225664 | tf_op jit(solution)/shard_map/yk,mkj->myj/dot_general | solution.py:66
  364.2 6.3 copy.76
  370.6 1.5 copy.83
  372.1 3.1 copy.85
  375.2 20.1 %fusion.60 = f32[1536,2048]{1,0:T(8,128)} fusion(s32[512]{0:T(512)S(1)} %iota_add_fusion, bf16[192,8,4,128]{3,2,1,0:T(4,128)(2,1)S(1)} %bitcast.298), kind=kOutput, calls=%fused_computation.89 | convolution fusion | flops 3238002688 | bytes 14157824 | tf_op jit(solution)/shard_map/dot_general | solution.py:75
  395.3 4.8 all-to-all-start.3
  400.2 22.3 %fusion = f32[1536,2048]{1,0:T(8,128)} fusion(f32[1536,2048]{1,0:T(8,128)} %fusion.60, s32[512]{0:T(512)S(1)} %iota_add_fusion, bf16[192,8,4,128]{3,2,1,0:T(4,128)(2,1)S(1)} %bitcast.297), kind=kOutput, calls=%fused_computation.7 | convolution fusion | flops 3247439872 | bytes 26740736 | tf_op jit(solution)/shard_map/dot_general | solution.py:75
  422.4 4.6 copy.75
  427.0 23.9 %fusion.17 = f32[3072,2048]{1,0:T(8,128)} fusion(bf16[384,8,4,128]{3,2,1,0:T(4,128)(2,1)S(1)} %bitcast.293, s32[512]{0:T(512)S(1)} %iota_add_fusion), kind=kOutput, calls=%fused_computation.42 | convolution fusion | flops 6459228160 | bytes 28313600 | tf_op jit(solution)/shard_map/dot_general | solution.py:75
  450.9 4.6 copy.77
  455.5 24.4 %subtract_convert_fusion = bf16[3072,2048]{1,0:T(8,128)(2,1)S(1)} fusion(f32[3072,2048]{1,0:T(8,128)} %fusion.17, bf16[384,8,4,128]{3,2,1,0:T(4,128)(2,1)S(1)} %bitcast.292, s32[512]{0:T(512)S(1)} %iota_add_fusion), kind=kOutput, calls=%fused_computation | convolution fusion | flops 6471811072 | bytes 40896512 | tf_op jit(solution)/shard_map/dot_general | solution.py:75
  479.9 9.4 %slice_convert_fusion.1 = (f32[1536,2048]{1,0:T(8,128)}, f32[1536,2048]{1,0:T(8,128)}) fusion(bf16[3072,2048]{1,0:T(8,128)(2,1)S(1)} %subtract_convert_fusion), kind=kLoop, calls=%fused_computation.9 | loop fusion | flops 6291456 | bytes 37748736 | tf_op jit(solution)/shard_map/convert_element_type | solution.py:134
  489.3 15.6 %fusion.24 = (bf16[1,1,512,2048]{3,2,1,0:T(8,128)(2,1)S(1)}, bf16[1,1,512,2048]{3,2,1,0:T(8,128)(2,1)S(1)}, bf16[1,1,512,2048]{3,2,1,0:T(8,128)(2,1)S(1)}, bf16[1,1,512,2048]{3,2,1,0:T(8,128)(2,1)}) fusion(f32[1536,2048]{1,0:T(8,128)} %get-tuple-element.20, f32[1536,2048]{1,0:T(8,128)} %get-tuple-element.21, f32[1536,2048]{1,0:T(8,128)} %fusion), kind=kLoop, calls=%fused_computation.52 | loop fusion | flops 16777216 | bytes 46137344 | tf_op jit(solution)/shard_map/stack | solution.py:160
  504.9 5.7 maximum_bitcast_fusion
  510.6 6.9 all-to-all-start.6
  517.6 93.2 %all-to-all-done.6 = bf16[1,4,512,2048]{3,2,0,1:T(8,128)(2,1)} async-done(((bf16[1,4,512,2048]{3,2,0,1:T(8,128)(2,1)}), bf16[1,4,512,2048]{3,2,0,1:T(8,128)(2,1)}, u32[]{:S(2)}, u32[]{:S(2)}) %all-to-all-start.6) | async-done | bytes 8388640 | tf_op jit(solution)/shard_map/all_to_all | solution.py:162
  610.8 21.3 %negate_convert_fusion = bf16[2048,512]{1,0:T(8,128)(2,1)S(1)} fusion(bf16[2048,2048]{1,0:T(8,128)(2,1)} %bitcast.37, s32[512]{0:T(512)S(1)} %iota_add_fusion), kind=kOutput, calls=%fused_computation.31 | convolution fusion | flops 4313841664 | bytes 10487808 | tf_op jit(solution)/shard_map/dot_general | solution.py:37
  632.1 1.1 reduce_sum.96
  633.3 2.1 copy.87
  635.4 3.7 all-to-all-start.7
  639.1 22.1 %convolution_convert_fusion = bf16[2048,512]{1,0:T(8,128)(2,1)} fusion(bf16[2048,2048]{1,0:T(8,128)(2,1)} %bitcast.37, s32[512]{0:T(512)S(1)} %iota_add_fusion), kind=kOutput, calls=%fused_computation.49 | convolution fusion | flops 4312793088 | bytes 10487808 | tf_op jit(solution)/shard_map/dot_general | solution.py:32
  661.2 2.4 reduce_sum.97
  663.6 2.1 copy.90
  665.7 3.5 all-to-all-start.8
  670.0 16.3 %fusion.40 = f32[2,128,512]{2,1,0:T(8,128)S(1)} fusion(bf16[2,2048,128]{1,2,0:T(8,128)(2,1)S(1)} %bitcast.299, s32[512]{0:T(512)S(1)} %iota_add_fusion), kind=kOutput, calls=%fused_computation.68 | convolution fusion | flops 553648128 | bytes 1574912 | tf_op jit(solution)/shard_map/yk,myj->mkj/dot_general | solution.py:49
  686.6 16.1 %fusion.42 = f32[2,128,512]{2,1,0:T(8,128)S(1)} fusion(bf16[2,2048,128]{1,2,0:T(8,128)(2,1)S(1)} %bitcast.301, s32[512]{0:T(512)S(1)} %iota_add_fusion), kind=kOutput, calls=%fused_computation.70 | convolution fusion | flops 553648128 | bytes 1574912 | tf_op jit(solution)/shard_map/yk,myj->mkj/dot_general | solution.py:52
  702.8 16.1 %fusion.102 = bf16[2,1,512,128]{2,3,0,1:T(8,128)(2,1)S(1)} fusion(f32[2,128,512]{2,1,0:T(8,128)S(1)} %fusion.40, bf16[2,2048,128]{1,2,0:T(8,128)(2,1)S(1)} %bitcast.302, s32[512]{0:T(512)S(1)} %iota_add_fusion, f32[512,128]{0,1:T(8,128)S(1)} %copy.93), kind=kOutput, calls=%fused_computation.107 | convolution fusion | flops 554041344 | bytes 2099200 | tf_op jit(solution)/shard_map/yk,myj->mkj/dot_general | solution.py:49
  718.8 16.1 %fusion.105 = bf16[2,1,512,128]{2,3,0,1:T(8,128)(2,1)S(1)} fusion(f32[2,128,512]{2,1,0:T(8,128)S(1)} %fusion.42, bf16[2,2048,128]{1,2,0:T(8,128)(2,1)S(1)} %bitcast.300, s32[512]{0:T(512)S(1)} %iota_add_fusion, f32[512,128]{0,1:T(8,128)S(1)} %copy.67), kind=kOutput, calls=%fused_computation.108 | convolution fusion | flops 554041344 | bytes 2099200 | tf_op jit(solution)/shard_map/yk,myj->mkj/dot_general | solution.py:52
  735.8 29.7 %all-reduce.2.cloned.1.call-done = bf16[1,2,2,512,128]{3,4,1,2,0:T(8,128)(2,1)} async-done(((bf16[1,2,2,512,128]{3,4,1,2,0:T(8,128)(2,1)}), bf16[1,2,2,512,128]{3,4,1,2,0:T(8,128)(2,1)}) %all-reduce.2.cloned.1.call-update) | async-done | bytes 524304 | tf_op jit(solution)/shard_map/psum | solution.py:171
  765.5 2.2 copy.94
  (74 shorter events, 9.7 us)
Async XLA Ops:
  6.5 1.8 copy-start.2
  10.6 16.8 %copy-start = (bf16[2,512,2048]{2,1,0:T(8,128)(2,1)}, bf16[2,512,2048]{2,1,0:T(8,128)(2,1)S(1)}, u32[]{:S(2)}) copy-start(bf16[2,512,2048]{2,1,0:T(8,128)(2,1)S(1)} %maximum_select_fusion) | copy-start | bytes 12582916
  29.5 42.5 %all-to-all-start.1 = ((bf16[2,512,512]{1,0,2:T(2,128)(2,1)}), bf16[2,512,512]{1,0,2:T(2,128)(2,1)S(1)}, u32[]{:S(2)}, u32[]{:S(2)}) async-start(bf16[2,512,512]{1,0,2:T(2,128)(2,1)} %copy.71), calls=%async_computation.1 | async-start | bytes 2097152 | tf_op jit(solution)/shard_map/all_to_all | solution.py:47
  33.9 21.0 %copy-start.13 = (f32[1,64]{1,0:T(1,128)S(1)}, f32[1,64]{1,0:T(1,128)}, u32[]{:S(2)}) copy-start(f32[1,64]{1,0:T(1,128)} %param.12) | copy-start | bytes 772
  33.9 21.0 %copy-start.14 = (f32[1,64]{1,0:T(1,128)S(1)}, f32[1,64]{1,0:T(1,128)}, u32[]{:S(2)}) copy-start(f32[1,64]{1,0:T(1,128)} %param.13) | copy-start | bytes 772
  34.0 21.0 %copy-start.15 = (s32[4]{0:T(128)S(1)}, s32[4]{0:T(128)}, u32[]{:S(2)}) copy-start(s32[4]{0:T(128)} %param.15) | copy-start | bytes 52
  34.0 21.7 %copy-start.7 = (s32[512,128]{1,0:T(8,128)S(1)}, s32[512,128]{1,0:T(8,128)}, u32[]{:S(2)}) copy-start(s32[512,128]{1,0:T(8,128)} %param.11) | copy-start | bytes 786436
  34.0 21.7 %copy-start.12 = (f32[64]{0:T(128)S(1)}, f32[64]{0:T(128)}, u32[]{:S(2)}) copy-start(f32[64]{0:T(128)} %param.14) | copy-start | bytes 772
  72.0 25.0 %all-to-all-start = ((bf16[2,512,512]{1,0,2:T(2,128)(2,1)}), bf16[2,512,512]{1,0,2:T(2,128)(2,1)S(1)}, u32[]{:S(2)}, u32[]{:S(2)}) async-start(bf16[2,512,512]{1,0,2:T(2,128)(2,1)} %copy.69), calls=%async_computation | async-start | bytes 2097152 | tf_op jit(solution)/shard_map/all_to_all | solution.py:46
  80.3 16.7 %copy-start.4 = (bf16[2,2048,128]{1,2,0:T(8,128)(2,1)}, bf16[2,2048,128]{1,2,0:T(8,128)(2,1)S(1)}, u32[]{:S(2)}) copy-start(bf16[2,2048,128]{1,2,0:T(8,128)(2,1)S(1)} %all_to_all.110) | copy-start | bytes 3145732
  98.6 1.0 copy-start.6
  99.6 16.5 %copy-start.16 = (f32[2,128,512]{2,1,0:T(8,128)S(1)}, f32[2,128,512]{2,1,0:T(8,128)}, u32[]{:S(2)}) copy-start(f32[2,128,512]{2,1,0:T(8,128)} %fusion.46) | copy-start | bytes 1572868
  116.1 17.3 %copy-start.5 = (bf16[2,2048,128]{1,2,0:T(8,128)(2,1)S(1)}, bf16[2,2048,128]{1,2,0:T(8,128)(2,1)}, u32[]{:S(2)}) copy-start(bf16[2,2048,128]{1,2,0:T(8,128)(2,1)} %copy-done.4) | copy-start | bytes 3145732
  149.2 35.8 %copy-start.1 = (f32[2,512,128]{1,2,0:T(8,128)}, f32[2,512,128]{1,2,0:T(8,128)S(1)}, u32[]{:S(2)}) copy-start(f32[2,512,128]{1,2,0:T(8,128)S(1)} %fusion.75) | copy-start | bytes 1572868
  149.6 0.9 copy-start.8
  150.5 0.9 copy-start.10
  237.8 50.1 %all-to-all-start.4 = ((bf16[3,2048,128]{2,0,1:T(4,128)(2,1)}), bf16[3,2048,128]{2,0,1:T(4,128)(2,1)S(1)}, u32[]{:S(2)}, u32[]{:S(2)}) async-start(bf16[3,2048,128]{2,0,1:T(4,128)(2,1)} %copy.82), calls=%async_computation.4 | async-start | bytes 4194304 | tf_op jit(solution)/shard_map/all_to_all | solution.py:69
  287.9 32.7 %all-to-all-start.5 = ((bf16[3,2048,128]{2,0,1:T(4,128)(2,1)}), bf16[3,2048,128]{2,0,1:T(4,128)(2,1)}, u32[]{:S(2)}, u32[]{:S(2)}) async-start(bf16[3,2048,128]{2,0,1:T(4,128)(2,1)} %copy.84), calls=%async_computation.5 | async-start | bytes 4194304 | tf_op jit(solution)/shard_map/all_to_all | solution.py:70
  320.6 5.2 copy-start.9
  320.6 74.7 %all-to-all-start.2 = ((bf16[6,2048,128]{2,0,1:T(8,128)(2,1)}), bf16[6,2048,128]{2,0,1:T(8,128)(2,1)}, u32[]{:S(2)}, u32[]{:S(2)}) async-start(bf16[6,2048,128]{2,0,1:T(8,128)(2,1)} %copy.74), calls=%async_computation.2 | async-start | bytes 8388608 | tf_op jit(solution)/shard_map/all_to_all | solution.py:69
  325.8 16.4 %copy-start.11 = (bf16[6,512,128]{1,2,0:T(8,128)(2,1)S(1)}, bf16[6,512,128]{1,2,0:T(8,128)(2,1)}, u32[]{:S(2)}) copy-start(bf16[6,512,128]{1,2,0:T(8,128)(2,1)} %get-tuple-element.33) | copy-start | bytes 2359300
  395.3 55.6 %all-to-all-start.3 = ((bf16[6,2048,128]{2,0,1:T(8,128)(2,1)}), bf16[6,2048,128]{2,0,1:T(8,128)(2,1)}, u32[]{:S(2)}, u32[]{:S(2)}) async-start(bf16[6,2048,128]{2,0,1:T(8,128)(2,1)} %copy.76), calls=%async_computation.3 | async-start | bytes 8388608 | tf_op jit(solution)/shard_map/all_to_all | solution.py:70
  510.6 100.2 %all-to-all-start.6 = ((bf16[1,4,512,2048]{3,2,0,1:T(8,128)(2,1)}), bf16[1,4,512,2048]{3,2,0,1:T(8,128)(2,1)}, u32[]{:S(2)}, u32[]{:S(2)}) async-start(bf16[1,4,512,2048]{3,2,0,1:T(8,128)(2,1)} %maximum_bitcast_fusion), calls=%async_computation.6 | async-start | bytes 16777216 | tf_op jit(solution)/shard_map/all_to_all | solution.py:162
  635.4 30.3 %all-to-all-start.7 = ((bf16[2,512,512]{1,0,2:T(2,128)(2,1)}), bf16[2,512,512]{1,0,2:T(2,128)(2,1)S(1)}, u32[]{:S(2)}, u32[]{:S(2)}) async-start(bf16[2,512,512]{1,0,2:T(2,128)(2,1)} %copy.87), calls=%async_computation.7 | async-start | bytes 2097152 | tf_op jit(solution)/shard_map/all_to_all | solution.py:47
  661.2 8.0 %copy-start.3 = (f32[512,128]{1,0:T(8,128)S(1)}, f32[512,128]{1,0:T(8,128)}, u32[]{:S(2)}) copy-start(f32[512,128]{1,0:T(8,128)} %get-tuple-element.5) | copy-start | bytes 786436
  665.7 20.7 %all-to-all-start.8 = ((bf16[2,512,512]{1,0,2:T(2,128)(2,1)}), bf16[2,512,512]{1,0,2:T(2,128)(2,1)S(1)}, u32[]{:S(2)}, u32[]{:S(2)}) async-start(bf16[2,512,512]{1,0,2:T(2,128)(2,1)} %copy.90), calls=%async_computation.8 | async-start | bytes 2097152 | tf_op jit(solution)/shard_map/all_to_all | solution.py:46
  669.2 96.3 %all-reduce.2.cloned.1.call-start = ((), (), s32[]{:S(2)}) async-start(), calls=%async_computation.9 | async-start | bytes 1048576 | tf_op jit(solution)/shard_map/psum | solution.py:171
Sparse Core Ops, SparseCore 0:
  735.9 29.5 all-reduce.1
where the time goes:
time: 784 us; the launch traced here: 775 us
  matrix products  448 us (57%)
  waiting for transfers between devices  123 us (16%)
  other arithmetic  61.5 us (8%)
  local copies, waits for them, and re-layouts  54.4 us (7%)
  starting transfers between devices  40.7 us (5%)
  blocking collectives  32.9 us (4%)
  between operations  14.3 us (2%)
    all_to_all x1, waiting for transfers between devices, body(): lax.all_to_all(products[None], 'field', split_axis=1, concat_axis=0, tile...  93.2 us
    dot_general x2, matrix products, inverse(): jnp.dot(flat_im, isin.T, preferred_element_type=jnp.float32)  46.6 us
    dot_general x2, matrix products, inverse(): jnp.dot(flat_re, icos.T, preferred_element_type=jnp.float32)  44 us
    dot_general x2, matrix products, column_part(): jnp.dot(flat, cos_t, preferred_element_type=jnp.float32)  41 us
    dot_general x2, matrix products, inverse(): jnp.einsum('yk,mkj->myj', isin, z_re, preferred_element_type=jnp.float32)  40.5 us
    dot_general x2, matrix products, column_part(): jnp.dot(flat, sin_t, preferred_element_type=jnp.float32)  38.1 us
    dot_general x2, matrix products, inverse(): jnp.einsum('yk,mkj->myj', isin, z_im, preferred_element_type=jnp.float32)  37.2 us
    dot_general x2, matrix products, inverse(): jnp.einsum('yk,mkj->myj', icos, z_re, preferred_element_type=jnp.float32)  36.1 us
  transfers between devices with their start and end apart: 10, of which 2 were waited for; matrix products, arithmetic and copies ran while one was open for 38% of the time, Pallas kernels for 0%

commit v1 on v0

v1 whole, which is shorter than its diff:
```python
import functools
import math

import jax
import jax.numpy as jnp
import numpy as np
from jax import lax
from jax.experimental import pallas as pl
from jax.experimental.pallas import tpu as pltpu
from jax.sharding import PartitionSpec as P

TILE = 128
BF = jnp.bfloat16
F32 = jnp.float32
VMEM_LIMIT = 60 * 1024 * 1024


def cis(pixels, freqs, npix):
    phase = jnp.mod(pixels[:, None] * freqs[None, :], npix)
    angle = phase.astype(F32) * (2.0 * math.pi / npix)
    return jnp.cos(angle), jnp.sin(angle)


def outer_cis(start, count, freqs, npix):
    low = 32
    freqs = jnp.asarray(freqs, jnp.int32)
    c1, s1 = cis(start + low * jnp.arange(count // low, dtype=jnp.int32), freqs, npix)
    c0, s0 = cis(jnp.arange(low, dtype=jnp.int32), freqs, npix)
    c1, s1, c0, s0 = lax.optimization_barrier((c1, s1, c0, s0))
    c1, s1, c0, s0 = c1[:, None], s1[:, None], c0[None], s0[None]
    width = freqs.shape[0]
    return (
        (c1 * c0 - s1 * s0).reshape(count, width),
        (s1 * c0 + c1 * s0).reshape(count, width),
    )


def lookup_kernel(idx_ref, tab_ref, *outs):
    idx = idx_ref[...].astype(jnp.int32)
    for t, out in enumerate(outs):
        table = jnp.broadcast_to(tab_ref[t : t + 1, :], idx.shape)
        out[...] = jnp.take_along_axis(table, idx, axis=1, mode="promise_in_bounds")


def lookup(idx, values):
    rows, width = idx.shape
    nbins = values[0].shape[0]
    tab = jnp.stack([jnp.pad(v, (0, 128 - nbins)) for v in values])
    tab = jnp.pad(tab, ((0, 8 - len(values)), (0, 0)))
    return pl.pallas_call(
        lookup_kernel,
        out_shape=[jax.ShapeDtypeStruct(idx.shape, F32) for _ in values],
        grid=(width // 128,),
        in_specs=[
            pl.BlockSpec((rows, 128), lambda i: (0, i)),
            pl.BlockSpec((8, 128), lambda i: (0, 0)),
        ],
        out_specs=[pl.BlockSpec((rows, 128), lambda i: (0, i)) for _ in values],
    )(idx, tab)


def ky_kernel(cols, x_ref, w_ref, gx_ref, gy_ref, t_ref, y_ref):
    half = x_ref.shape[2] // 2
    top = y_ref.shape[2] // 2
    x = x_ref[0, 0].astype(F32)
    wide = x.shape[1]
    lane = lax.broadcasted_iota(jnp.int32, x.shape, 1)
    first = (lane & (cols - 1)) < cols // 2
    ix = jnp.where(
        first, -pltpu.roll(x, wide - cols // 2, axis=1), pltpu.roll(x, cols // 2, axis=1)
    )
    w, gx, gy = w_ref[0], gx_ref[0], gy_ref[0]
    pairs = ((w * x, w * ix), (gx * ix, -(gx * x)), (gy * ix, -(gy * x)))
    for leg, (z, iz) in enumerate(pairs):
        z = z.astype(BF)
        iz = iz.astype(BF)
        even = jnp.dot(
            t_ref[0], jnp.concatenate([z[:half], iz[:half]], axis=0), preferred_element_type=F32
        )
        odd = jnp.dot(
            t_ref[1], jnp.concatenate([z[half:], iz[half:]], axis=0), preferred_element_type=F32
        )
        y_ref[0, leg, :top, :] = (even + odd).astype(BF)
        y_ref[0, leg, top:, :] = (even - odd).astype(BF)


def ky_inverse(x, w, gx, gy, table, cols):
    maps, _, kf, wide = x.shape
    top = table.shape[1]
    lanes = 256
    blocks = wide // lanes
    cell = pl.BlockSpec((1, kf, lanes), lambda p, i, m: (p, 0, i))
    return pl.pallas_call(
        functools.partial(ky_kernel, cols),
        out_shape=jax.ShapeDtypeStruct((maps, 3, 2 * top, 2 * wide), BF),
        grid=(2, blocks, maps),
        in_specs=[
            pl.BlockSpec((1, 1, kf, lanes), lambda p, i, m: (m, p, 0, i)),
            cell,
            cell,
            cell,
            pl.BlockSpec(table.shape, lambda p, i, m: (0, 0, 0)),
        ],
        out_specs=pl.BlockSpec(
            (1, 3, 2 * top, lanes), lambda p, i, m: (m, 0, 0, p * blocks + i)
        ),
        compiler_params=pltpu.CompilerParams(vmem_limit_bytes=VMEM_LIMIT),
    )(x, w, gx, gy, table)


def pixel_kernel(xt, y_ref, yp_ref, f_ref, a_ref, legs, prods):
    step = pl.program_id(0)
    height = y_ref.shape[2]
    wide = f_ref.shape[2]
    here = pl.ds(pl.multiple_of(step * xt, xt), xt)
    dims = (((1,), (1,)), ((), ()))

    def make(source, m, leg, slot):
        even = lax.dot_general(
            source[m, leg, :, :wide], f_ref[0, here, :], dims, preferred_element_type=F32
        )
        odd = lax.dot_general(
            source[m, leg, :, wide:], f_ref[1, here, :], dims, preferred_element_type=F32
        )
        legs[0, slot] = (even + odd).astype(BF)
        legs[1, slot] = (even - odd).astype(BF)

    @pl.loop(0, 3)
    def _(leg):
        make(y_ref, 0, leg, leg)
        make(y_ref, 1, leg, leg + 3)
        make(yp_ref, 0, leg, leg + 6)

    chunk = 64

    @pl.loop(0, height // chunk)
    def _(c):
        rows = pl.ds(pl.multiple_of(c * chunk, chunk), chunk)
        sides = []
        for side in range(2):
            own = [legs[side, i, rows, :].astype(F32) for i in range(3)]
            dat = [legs[side, i + 3, rows, :].astype(F32) for i in range(3)]
            par = [legs[side, i + 6, rows, :].astype(F32) for i in range(3)]
            sides.append(
                (
                    dat[1] * own[0] + own[1] * dat[0],
                    own[1] * par[0] + par[1] * own[0],
                    dat[2] * own[0] + own[2] * dat[0],
                    own[2] * par[0] + par[2] * own[0],
                )
            )
        for i in range(4):
            prods[0, i, rows, here] = (sides[0][i] + sides[1][i]).astype(BF)
            prods[1, i, rows, here] = (sides[0][i] - sides[1][i]).astype(BF)

    @pl.when(step == pl.num_programs(0) - 1)
    def _():
        @pl.loop(0, 4)
        def _(i):
            for p in range(2):
                where = pl.ds(pl.multiple_of(i * (2 * wide) + p * wide, wide), wide)
                a_ref[:, where] = jnp.dot(
                    prods[p, i], f_ref[p], preferred_element_type=F32
                ).astype(BF)


def pixel_products(y, yp, table):
    height = y.shape[2]
    pixels, wide = table.shape[1:]
    xt = 256
    whole = lambda a: pl.BlockSpec(
        a.shape, lambda i: (0,) * a.ndim, pipeline_mode=pl.Buffered(1)
    )
    return pl.pallas_call(
        functools.partial(pixel_kernel, xt),
        out_shape=jax.ShapeDtypeStruct((height, 8 * wide), BF),
        grid=(pixels // xt,),
        in_specs=[whole(y), whole(yp), whole(table)],
        out_specs=pl.BlockSpec((height, 8 * wide), lambda i: (0, 0)),
        scratch_shapes=[
            pltpu.VMEM((2, 9, height, xt), BF),
            pltpu.VMEM((2, 4, height, pixels), BF),
        ],
        compiler_params=pltpu.CompilerParams(vmem_limit_bytes=VMEM_LIMIT),
    )(y, yp, table)


def body(nrows, nreal, nfield, sims, data, mask_flags, bins, cl_signal, cl_noise, norm, matching):
    height, npix = sims.shape[2:]
    kf, cols = bins.shape
    half, kh, jc = npix // 2, kf // 2, cols // 2
    top = height // 2
    row = lax.axis_index("rows")
    forward_scale = npix ** (-0.5)
    inverse_gain = kf ** (-0.5) / forward_scale

    freq = np.arange(kf) - kf // 2
    lanes_k, lanes_c = [], np.tile(np.repeat(np.arange(2), jc), nrows)
    for p in range(2):
        per_q = freq[p::2].reshape(nrows, 1, jc)
        lanes_k.append(np.broadcast_to(per_q, (nrows, 2, jc)).reshape(-1))
    ky_order = np.concatenate([freq[0::2], freq[1::2]])

    fx = []
    for p in range(2):
        c, s = outer_cis(0, half, lanes_k[p], npix)
        fx.append((jnp.where(lanes_c[None, :] == 0, c, -s) * forward_scale).astype(BF))
    fx = jnp.stack(fx)
    c, s = outer_cis(0, npix, ky_order, npix)
    cs = (jnp.concatenate([c, s], axis=1) * forward_scale).astype(BF)
    c, s = outer_cis(row * top, top, ky_order, npix)
    c = (c * forward_scale).astype(BF)
    s = (s * forward_scale).astype(BF)
    gain = jnp.asarray(inverse_gain * inverse_gain, BF)
    t8 = jnp.stack([jnp.concatenate([c[:, :kh], s[:, :kh]], axis=1),
                    jnp.concatenate([c[:, kh:], s[:, kh:]], axis=1)]) * gain
    c, s = outer_cis(row * top, top, freq, npix)
    local = (jnp.concatenate([c, s], axis=1) * forward_scale).astype(BF)
    sign = jnp.asarray(np.tile(1 - 2 * (freq % 2), 2)[None, :], BF)
    local = jnp.concatenate([local, local * sign], axis=0)
    fx, cs, t8, local = lax.optimization_barrier((fx, cs, t8, local))

    pick = np.zeros((cols, 2, 2, jc), np.float32)
    for p in range(2):
        for j in range(jc):
            pick[2 * j + p, p, :, j] = 1.0
    swap = np.zeros((kf, kf), np.float32)
    swap[np.arange(kf), ky_order + kf // 2] = 1.0
    moved = jnp.dot(jnp.asarray(swap, BF), bins.astype(BF), preferred_element_type=F32).astype(BF)
    moved = jnp.dot(
        moved, jnp.asarray(pick.reshape(cols, 4 * jc), BF), preferred_element_type=F32
    ).astype(BF)
    moved = moved.reshape(kf, 2, cols).transpose(1, 0, 2)
    cells = lax.all_gather(moved, "rows", axis=2, tiled=True)
    weight_vals = 1.0 / (cl_signal[0] + cl_noise[0])
    grad_vals = cl_signal[0] * weight_vals
    w, g = lookup(cells.reshape(2 * kf, kf), [weight_vals, grad_vals])
    w = w.reshape(2, kf, kf)
    g = g.reshape(2, kf, kf)
    step_size = 2.0 * math.pi / npix
    lx = jnp.asarray(np.stack(lanes_k)[:, None, :] * step_size, F32)
    ly = jnp.asarray(ky_order[None, :, None] * step_size, F32)
    gx, gy = lx * g, ly * g
    flat_bins = bins.reshape(-1, 128)
    ncell = lookup(flat_bins, [norm])[0].reshape(kf, cols)

    mask = jnp.repeat(jnp.repeat(mask_flags, TILE, axis=0), TILE, axis=1) > 0
    stacked = jnp.concatenate([sims[0], data], axis=0)
    masked = jnp.where(mask[None], stacked, jnp.zeros_like(stacked))
    lo, hi = masked[:, :, :half], masked[:, :, half:]
    flat = lambda a: a.reshape(2 * height, half)
    parts = [
        jnp.dot(flat(lo + hi), fx[0], preferred_element_type=F32).astype(BF),
        jnp.dot(flat(lo - hi), fx[1], preferred_element_type=F32).astype(BF),
    ]
    a = jnp.stack([v.reshape(2, height, nrows, cols) for v in parts])
    a = a.transpose(3, 2, 1, 0, 4).reshape(nrows * height, 4 * cols)
    a = lax.all_to_all(a, "rows", split_axis=0, concat_axis=0, tiled=True)
    pq = lax.dot_general(cs, a, (((0,), (0,)), ((), ())), preferred_element_type=F32)
    pq = pq.reshape(2, kf, 2, 2, 2, jc)
    x = jnp.stack(
        [pq[0, ..., 0, :] + pq[1, ..., 1, :], pq[0, ..., 1, :] - pq[1, ..., 0, :]], axis=3
    )
    x = x.astype(BF).transpose(1, 2, 0, 3, 4).reshape(2, 2, kf, cols)

    real = lax.axis_index("real")
    ids = jnp.arange(nreal, dtype=jnp.int32)
    partner = jnp.sum(jnp.where(ids == real, matching, 0))
    px = x[0]
    for shift in range(1, nreal):
        came = lax.ppermute(
            x[0], "real", [((d + shift) % nreal, d) for d in range(nreal)]
        )
        px = jnp.where(lax.rem(real + shift, nreal) == partner, came, px)

    both = lax.all_gather(x, "rows", axis=3, tiled=True)
    y = ky_inverse(both, w, gx, gy, t8, cols)
    other = lax.all_gather(px[None], "rows", axis=3, tiled=True)
    yp = ky_inverse(other, w, gx, gy, t8, cols)
    field_a = pixel_products(y, yp, fx)

    sums = lax.dot_general(local, field_a, (((0,), (0,)), ((), ())), preferred_element_type=F32)
    sums = sums.reshape(2, kf, 2, 2, 2, nrows, 2, jc)
    s_re = sums[0, ..., 0, :] + sums[1, ..., 1, :]
    s_im = sums[0, ..., 1, :] - sums[1, ..., 0, :]
    lxo = jnp.asarray(
        np.stack([freq[p::2] for p in range(2)]).reshape(1, 1, 2, nrows, jc) * step_size, F32
    )
    lyo = jnp.asarray(freq.reshape(kf, 1, 1, 1, 1) * step_size, F32)
    terms = jnp.stack(
        [
            -(lxo * s_im[:, 0] + lyo * s_im[:, 1]),
            lxo * s_re[:, 0] + lyo * s_re[:, 1],
        ],
        axis=2,
    ).astype(BF)
    terms = terms.transpose(4, 1, 2, 0, 3, 5).reshape(nrows * 4 * kf, cols)
    order = np.zeros((2, jc, cols), np.float32)
    for p in range(2):
        order[p, np.arange(jc), 2 * np.arange(jc) + p] = 1.0
    terms = jnp.dot(
        terms, jnp.asarray(order.reshape(cols, cols), BF), preferred_element_type=F32
    ).astype(BF)
    got = lax.all_to_all(terms, "rows", split_axis=0, concat_axis=0, tiled=True)
    got = jnp.sum(got.reshape(nrows, 2, 2, kf, cols).astype(F32), axis=0)
    mine = (got * ncell).astype(BF)
    total = mine.astype(F32)
    for shift in range(1, nfield):
        theirs = lax.ppermute(
            mine, "field", [(d, (d + shift) % nfield) for d in range(nfield)]
        )
        total = total + theirs.astype(F32)
    return total[None]


def solution(mesh):
    in_specs = (
        P("real", "field", "rows", None),
        P("field", "rows", None),
        P("rows", None),
        P(None, "rows"),
        P("field", None),
        P("field", None),
        P(),
        P(),
    )
    out_specs = P("real", None, None, None, "rows")
    f = functools.partial(body, mesh.shape["rows"], mesh.shape["real"], mesh.shape["field"])
    return jax.shard_map(f, mesh=mesh, in_specs=in_specs, out_specs=out_specs, check_vma=False)
```

time: 784 us -> 306 us (0.39); the launches traced: 775 us -> 305 us
  matrix products: 448 us -> 22.6 us
  Pallas kernels: 0 us -> 53.5 us
  blocking collectives: 32.9 us -> 0 us
  starting transfers between devices: 40.7 us -> 16.1 us
  waiting for transfers between devices: 123 us -> 99.2 us
  other arithmetic: 61.5 us -> 45.4 us
    dot_general x24 -> x6, matrix products: 448 us -> 22.6 us  [the longest x1 10.4 us: body(): lax.dot_general(local, field_a, (((0,), (0,)), ((), ())), preferred_eleme...]
    pallas_call x0 -> x5, Pallas kernels: none -> 53.5 us  [the longest x1 27.5 us: pixel_products(): pl.pallas_call(functools.partial(pixel_kernel, xt), out_shape=jax.ShapeDt...]
    all_to_all x9 -> x2, waiting for transfers between devices: 93.3 us -> 46.4 us  [the longest x1 23.3 us: body(): a = lax.all_to_all(a, 'rows', split_axis=0, concat_axis=0, tiled=True)]
    all_gather x2 -> x0, blocking collectives: 32.9 us -> none  [the longest x1 17.2 us: body(): lax.all_gather(x_re[0:1].astype(jnp.bfloat16), 'real', axis=0, tiled=True)]
    all_to_all x9 -> x2, starting transfers between devices: 40.6 us -> 8.11 us  [the longest x1 4.37 us: body(): a = lax.all_to_all(a, 'rows', split_axis=0, concat_axis=0, tiled=True)]
    psum x1 -> x0, waiting for transfers between devices: 29.7 us -> none  [body(): total = lax.psum(terms.astype(jnp.bfloat16), 'field').astype(jnp.float32)]
    all_gather x0 -> x3, waiting for transfers between devices: none -> 27.4 us  [the longest x1 17.6 us: body(): both = lax.all_gather(x, 'rows', axis=3, tiled=True)]
    ppermute x0 -> x4, waiting for transfers between devices: none -> 25.3 us  [the longest x3 13.3 us: body(): lax.ppermute(x[0], 'real', [((d + shift) % nreal, d) for d in range(nreal)])]
  transfers between devices with their start and end apart: 10 -> 9, of which waited for: 2 -> 7; matrix products, arithmetic and copies ran while one was open for 38% -> 8% of each run, Pallas kernels for 0% -> 5%
where the time goes in v1:
time: 306 us; the launch traced here: 305 us
  waiting for transfers between devices  99.2 us (32%)
  Pallas kernels  53.5 us (17%)
  local copies, waits for them, and re-layouts  52.6 us (17%)
  other arithmetic  45.4 us (15%)
  matrix products  22.6 us (7%)
  starting transfers between devices  16.1 us (5%)
  between operations  15.3 us (5%)
    pallas_call x1, Pallas kernels, pixel_products(): pl.pallas_call(functools.partial(pixel_kernel, xt), out_shape=jax.ShapeDt...  27.5 us
    all_to_all x1, waiting for transfers between devices, body(): a = lax.all_to_all(a, 'rows', split_axis=0, concat_axis=0, tiled=True)  23.3 us
    all_to_all x1, waiting for transfers between devices, body(): got = lax.all_to_all(terms, 'rows', split_axis=0, concat_axis=0, tiled=True)  23.1 us
    reshape x1, local copies, waits for them, and re-layouts, body(): sums = sums.reshape(2, kf, 2, 2, 2, nrows, 2, jc)  22 us
    pallas_call x2, Pallas kernels, ky_inverse(): pl.pallas_call(functools.partial(ky_kernel, cols), out_shape=jax.ShapeDty...  18.8 us
    slice x1, other arithmetic, body(): s_im = sums[0, ..., 1, :] - sums[1, ..., 0, :]  17.9 us
    all_gather x1, waiting for transfers between devices, body(): both = lax.all_gather(x, 'rows', axis=3, tiled=True)  17.6 us
    ppermute x3, waiting for transfers between devices, body(): lax.ppermute(x[0], 'real', [((d + shift) % nreal, d) for d in range(nreal)])  13.3 us
  transfers between devices with their start and end apart: 9, of which 7 were waited for; matrix products, arithmetic and copies ran while one was open for 8% of the time, Pallas kernels for 5%

profile of v1, /device:TPU:0, one launch (start us, length us, event | category | flops | bytes accessed | tf_op | source)
XLA Modules:
  0.0 304.7 jit_solution(7496208558858429994)
XLA Ops:
  6.6 1.0 fusion.64
  7.6 1.0 fusion.62
  8.5 0.9 fusion.80
  9.7 1.1 fusion.70
  10.7 0.6 fusion.52
  11.4 0.9 maximum_multiply_fusion.2.t_ref
  12.2 1.3 multiply_subtract_fusion.1
  13.6 1.2 fusion.14
  15.1 0.3 copy-done.14
  15.7 1.0 pad_maximum_fusion.2
  16.7 1.2 multiply_subtract_fusion
  17.9 2.8 fusion
  20.7 3.5 %broadcast_in_dim.40 = pred[512,16,128]{2,1,0:T(8,128)(4,1)S(1)} broadcast(pred[512,16]{1,0:T(8,128)(4,1)S(1)} %bitcast.187), dimensions={0,1} | broadcast | bytes 1056768 | tf_op jit(solution)/shard_map/broadcast_in_dim | solution.py:247
  24.2 0.6 copy.86
  24.9 1.0 maximum_select_fusion
  25.8 1.6 slice_add_fusion.1
  27.5 2.2 convolution_convert_fusion.2
  29.7 1.3 stack_reshape.6
  31.0 1.5 copy.51
  32.5 2.8 convolution_convert_fusion.1
  35.3 0.3 stack_reshape.7
  35.6 0.7 copy.52
  36.6 1.5 pad_maximum_fusion.1
  38.1 4.4 %all-to-all-start = ((bf16[4,512,512]{1,2,0:T(8,128)(2,1)}), bf16[4,512,512]{1,2,0:T(8,128)(2,1)S(1)}, u32[]{:S(2)}, u32[]{:S(2)}) async-start(bf16[4,512,512]{1,2,0:T(8,128)(2,1)} %bitcast.161), calls=%async_computation | async-start | bytes 4194304 | tf_op jit(solution)/shard_map/all_to_all | solution.py:258
  42.5 0.6 convolution_convert_fusion.3
  43.1 0.8 copy.60
  44.0 6.5 %copy.72 = bf16[1024,2048]{1,0:T(8,128)(2,1)} copy(bf16[1024,2048]{0,1:T(8,128)(2,1)} %bitcast.155) | data formatting | bytes 8388608 | tf_op jit(solution)/shard_map/dot_general | solution.py:259
  50.5 23.3 %all-to-all-done = bf16[4,512,512]{1,2,0:T(8,128)(2,1)S(1)} async-done(((bf16[4,512,512]{1,2,0:T(8,128)(2,1)}), bf16[4,512,512]{1,2,0:T(8,128)(2,1)S(1)}, u32[]{:S(2)}, u32[]{:S(2)}) %all-to-all-start) | async-done | bytes 2097184 | tf_op jit(solution)/shard_map/all_to_all | solution.py:258
  73.8 2.4 copy.53
  76.2 2.9 copy.54
  79.1 4.5 %fusion.91 = f32[2,512,2,2,2,64]{1,5,4,3,2,0:T(8,128)S(1)} fusion(bf16[2,512,2048,1,1,1]{2,1,5,4,3,0:T(8,128)(2,1)} %bitcast.170, bf16[2,2,2,64,2048,1]{4,3,2,1,0,5:T(8,128)(2,1)S(1)} %bitcast.175), kind=kOutput, calls=%fused_computation.185 | convolution fusion | flops 2147483648 | bytes 8388608 | tf_op jit(solution)/shard_map/dot_general | solution.py:259
  84.1 2.4 collective-permute-start
  86.5 2.6 collective-permute-start.1
  89.1 1.4 collective-permute-start.2
  90.5 0.6 fusion.84
  92.8 3.1 %collective-permute-done = bf16[2,512,128]{2,1,0:T(8,128)(2,1)S(1)} collective-permute-done((bf16[2,512,128]{2,1,0:T(8,128)(2,1)S(1)}, bf16[2,512,128]{2,1,0:T(8,128)(2,1)S(1)}, u32[]{:S(2)}, u32[]{:S(2)}) %collective-permute-start) | collective-permute-done | bytes 262176 | tf_op jit(solution)/shard_map/ppermute | solution.py:271
  95.9 10.2 %collective-permute-done.1 = bf16[2,512,128]{2,1,0:T(8,128)(2,1)S(1)} collective-permute-done((bf16[2,512,128]{2,1,0:T(8,128)(2,1)S(1)}, bf16[2,512,128]{2,1,0:T(8,128)(2,1)S(1)}, u32[]{:S(2)}, u32[]{:S(2)}) %collective-permute-start.1) | collective-permute-done | bytes 262176 | tf_op jit(solution)/shard_map/ppermute | solution.py:271
  106.0 0.8 select_select_fusion
  106.9 1.0 copy.59
  108.0 0.6 select_maximum_fusion.tab_ref
  108.6 5.3 %shard_map.217 = (f32[1024,512]{1,0:T(8,128)}, f32[1024,512]{1,0:T(8,128)}) custom-call(bf16[1024,512]{1,0:T(8,128)(2,1)} %bitcast.181, f32[8,128]{1,0:T(8,128)} %select_maximum_fusion.tab_ref), custom_call_target="tpu_custom_call" | custom-call | tf_op jit(solution)/shard_map/pallas_call | solution.py:50
  113.9 3.9 %broadcast_multiply_fusion = (f32[2,512,512]{2,1,0:T(8,128)}, f32[2,512,512]{2,1,0:T(8,128)}) fusion(f32[2,512,512]{2,1,0:T(8,128)} %bitcast.172, f32[512]{0:T(512)S(1)} %copy-done.13, f32[2,512]{1,0:T(2,128)S(1)} %copy-done.12), kind=kLoop, calls=%fused_computation.51 | loop fusion | flops 1048576 | bytes 6297600 | tf_op jit(solution)/shard_map/mul | solution.py:243
  117.8 9.9 %all-gather.9.cloned.1.call-done = bf16[2,512,512]{2,1,0:T(8,128)(2,1)} async-done(((bf16[2,512,128]{2,1,0:T(8,128)(2,1)}), bf16[2,512,512]{2,1,0:T(8,128)(2,1)}) %all-gather.9.cloned.1.call-update) | async-done | bytes 1048592 | tf_op jit(solution)/shard_map/all_gather | solution.py:278
  127.7 6.9 %shard_map.219.yp_ref = bf16[1,3,512,1024]{3,2,1,0:T(8,128)(2,1)} custom-call(bf16[1,2,512,512]{3,2,1,0:T(8,128)(2,1)} %bitcast.186, f32[2,512,512]{2,1,0:T(8,128)} %bitcast.167, f32[2,512,512]{2,1,0:T(8,128)} %get-tuple-element.67.gx_ref, f32[2,512,512]{2,1,0:T(8,128)} %get-tuple-element.66.gy_ref, bf16[2,256,512]{2,1,0:T(8,128)(2,1)} %maximum_multiply_fusion.2.t_ref), custom_call_target="tpu_custom_call" | custom-call | tf_op jit(solution)/shard_map/pallas_call | solution.py:93
  134.6 17.6 %all-gather.5.cloned.1.call-done.x_ref = bf16[2,2,512,512]{3,2,1,0:T(8,128)(2,1)} async-done(((bf16[2,2,512,128]{3,2,1,0:T(8,128)(2,1)}), bf16[2,2,512,512]{3,2,1,0:T(8,128)(2,1)}) %all-gather.5.cloned.1.call-update) | async-done | bytes 2097168 | tf_op jit(solution)/shard_map/all_gather | solution.py:276
  152.1 11.9 %shard_map.218.y_ref = bf16[2,3,512,1024]{3,2,1,0:T(8,128)(2,1)} custom-call(bf16[2,2,512,512]{3,2,1,0:T(8,128)(2,1)} %all-gather.5.cloned.1.call-done.x_ref, f32[2,512,512]{2,1,0:T(8,128)} %bitcast.168, f32[2,512,512]{2,1,0:T(8,128)} %get-tuple-element.67.gx_ref, f32[2,512,512]{2,1,0:T(8,128)} %get-tuple-element.66.gy_ref, ...), custom_call_target="tpu_custom_call" | custom-call | tf_op jit(solution)/shard_map/pallas_call | solution.py:93
  164.0 27.5 %shard_map.220 = bf16[512,4096]{1,0:T(8,128)(2,1)} custom-call(bf16[2,3,512,1024]{3,2,1,0:T(8,128)(2,1)} %shard_map.218.y_ref, bf16[1,3,512,1024]{3,2,1,0:T(8,128)(2,1)} %shard_map.219.yp_ref, bf16[2,1024,512]{2,1,0:T(8,128)(2,1)} %copy-done), custom_call_target="tpu_custom_call" | custom-call | tf_op jit(solution)/shard_map/pallas_call | solution.py:174
  191.6 10.4 %fusion.92 = f32[1024,4096]{0,1:T(8,128)} fusion(bf16[512,1024]{1,0:T(8,128)(2,1)S(1)} %copy-done.6, bf16[512,4096]{1,0:T(8,128)(2,1)} %shard_map.220), kind=kOutput, calls=%fused_computation.186 | convolution fusion | flops 4294967296 | bytes 22020096 | tf_op jit(solution)/shard_map/dot_general | solution.py:282
  201.9 22.0 %reshape.495 = f32[2,512,2,2,2,4,2,64]{1,0,7,6,5,4,3,2:T(2,128)} reshape(f32[1024,4096]{0,1:T(8,128)} %fusion.92) | data formatting | bytes 33554432 | tf_op jit(solution)/shard_map/reshape | solution.py:283
  223.9 17.9 %fusion.88 = (f32[1,512,2,2,2,4,1,64]{1,0,7,6,5,4,3,2:T(1,128)S(1)}, f32[1,512,2,2,2,4,1,64]{1,0,7,6,5,4,3,2:T(1,128)S(1)}, f32[1,512,2,2,2,4,1,64]{1,0,7,6,5,4,3,2:T(1,128)S(1)}) fusion(f32[2,512,2,2,2,4,2,64]{1,0,7,6,5,4,3,2:T(2,128)} %reshape.495), kind=kLoop, calls=%fused_computation.182 | loop fusion | flops 1048576 | bytes 29360128 | tf_op jit(solution)/shard_map/slice | solution.py:285
  241.9 0.7 copy.85
  242.5 1.3 fusion.1
  243.9 0.6 fusion.9
  244.7 3.5 %copy.69 = bf16[4,2,2,512,2,64]{3,2,1,0,5,4:T(2,128)(2,1)} copy(bf16[4,2,2,512,2,64]{3,5,0,4,1,2:T(8,128)(2,1)S(1)} %maximum_bitcast_fusion) | data formatting | bytes 4194304 | tf_op jit(solution)/shard_map/transpose | solution.py:297
  248.3 3.3 %reshape.496 = bf16[8192,128]{0,1:T(8,128)(2,1)S(1)} reshape(bf16[4,2,2,512,2,64]{3,2,1,0,5,4:T(2,128)(2,1)} %copy.69) | data formatting | bytes 4194304 | tf_op jit(solution)/shard_map/reshape | solution.py:297
  251.6 2.1 convolution_convert_fusion
  253.7 3.7 %all-to-all-start.1 = ((bf16[4,2048,128]{2,1,0:T(8,128)(2,1)}), bf16[4,2048,128]{2,1,0:T(8,128)(2,1)S(1)}, u32[]{:S(2)}, u32[]{:S(2)}) async-start(bf16[4,2048,128]{2,1,0:T(8,128)(2,1)} %bitcast.49), calls=%async_computation.1 | async-start | bytes 4194304 | tf_op jit(solution)/shard_map/all_to_all | solution.py:304
  257.5 0.6 pad.22.tab_ref
  258.1 1.9 shard_map.221
  260.0 23.1 %all-to-all-done.1 = bf16[4,2048,128]{2,1,0:T(8,128)(2,1)S(1)} async-done(((bf16[4,2048,128]{2,1,0:T(8,128)(2,1)}), bf16[4,2048,128]{2,1,0:T(8,128)(2,1)S(1)}, u32[]{:S(2)}, u32[]{:S(2)}) %all-to-all-start.1) | async-done | bytes 2097184 | tf_op jit(solution)/shard_map/all_to_all | solution.py:304
  283.1 0.3 convert_reduce_fusion
  283.5 1.5 collective-permute-start.3
  285.1 12.0 %collective-permute-done.3 = bf16[2,2,512,128]{3,2,1,0:T(8,128)(2,1)S(1)} collective-permute-done((bf16[2,2,512,128]{3,2,1,0:T(8,128)(2,1)S(1)}, bf16[2,2,512,128]{3,2,1,0:T(8,128)(2,1)S(1)}, u32[]{:S(2)}, u32[]{:S(2)}) %collective-permute-start.3) | collective-permute-done | bytes 524320 | tf_op jit(solution)/shard_map/ppermute | solution.py:309
  297.1 1.1 add_bitcast_fusion
  (79 shorter events, 2.0 us)
Async XLA Ops:
  6.5 4.2 %copy-start.10 = (s32[512]{0:T(512)S(1)}, s32[512]{0:T(512)}, u32[]{:S(2)}) copy-start(s32[512]{0:T(512)} %constant.143.clone) | copy-start | bytes 6148
  6.5 3.1 %copy-start.15 = (s32[512]{0:T(512)S(1)}, s32[512]{0:T(512)}, u32[]{:S(2)}) copy-start(s32[512]{0:T(512)} %constant.140.clone) | copy-start | bytes 6148
  6.5 3.1 %copy-start.16 = (s32[512]{0:T(512)S(1)}, s32[512]{0:T(512)}, u32[]{:S(2)}) copy-start(s32[512]{0:T(512)} %constant.142.clone) | copy-start | bytes 6148
  12.2 1.3 copy-start.21
  14.8 0.7 copy-start.14
  15.0 17.5 %copy-start = (bf16[2,1024,512]{2,1,0:T(8,128)(2,1)}, bf16[2,1024,512]{2,1,0:T(8,128)(2,1)S(1)}, u32[]{:S(2)}) copy-start(bf16[2,1024,512]{2,1,0:T(8,128)(2,1)S(1)} %pad_maximum_fusion.f_ref) | copy-start | bytes 6291460
  17.9 2.8 copy-start.17
  17.9 6.9 %copy-start.4 = (bf16[1,1,512,2048]{3,2,1,0:T(8,128)(2,1)S(1)}, bf16[1,1,512,2048]{3,2,1,0:T(8,128)(2,1)}, u32[]{:S(2)}) copy-start(bf16[1,1,512,2048]{3,2,1,0:T(8,128)(2,1)} %param.23) | copy-start | bytes 6291460
  20.7 4.2 %copy-start.3 = (bf16[1,512,2048]{2,1,0:T(8,128)(2,1)S(1)}, bf16[1,512,2048]{2,1,0:T(8,128)(2,1)}, u32[]{:S(2)}) copy-start(bf16[1,512,2048]{2,1,0:T(8,128)(2,1)} %param.24) | copy-start | bytes 6291460
  35.3 1.2 copy-start.1
  38.1 4.4 %copy-start.5 = (s32[512,128]{1,0:T(8,128)S(1)}, s32[512,128]{1,0:T(8,128)}, u32[]{:S(2)}) copy-start(s32[512,128]{1,0:T(8,128)} %idx_ref.1) | copy-start | bytes 786436
  38.1 4.4 %copy-start.7 = (bf16[512,512]{1,0:T(8,128)(2,1)S(1)}, bf16[512,512]{1,0:T(8,128)(2,1)}, u32[]{:S(2)}) copy-start(bf16[512,512]{1,0:T(8,128)(2,1)} %constant.146.clone) | copy-start | bytes 1572868
  38.1 4.4 %copy-start.8 = (bf16[128,256]{1,0:T(8,128)(2,1)S(1)}, bf16[128,256]{1,0:T(8,128)(2,1)}, u32[]{:S(2)}) copy-start(bf16[128,256]{1,0:T(8,128)(2,1)} %constant.147.clone) | copy-start | bytes 196612
  38.1 35.7 %all-to-all-start = ((bf16[4,512,512]{1,2,0:T(8,128)(2,1)}), bf16[4,512,512]{1,2,0:T(8,128)(2,1)S(1)}, u32[]{:S(2)}, u32[]{:S(2)}) async-start(bf16[4,512,512]{1,2,0:T(8,128)(2,1)} %bitcast.161), calls=%async_computation | async-start | bytes 4194304 | tf_op jit(solution)/shard_map/all_to_all | solution.py:258
  42.5 66.1 %all-gather.7.cloned.1.call-start = ((), (), s32[]{:S(2)}) async-start(), calls=%async_computation.3 | async-start | bytes 1310720 | tf_op jit(solution)/shard_map/all_gather | solution.py:234
  43.9 83.8 %all-gather.9.cloned.1.call-start = ((), (), s32[]{:S(2)}) async-start(), calls=%async_computation.4 | async-start | bytes 1310720 | tf_op jit(solution)/shard_map/all_gather | solution.py:278
  83.7 6.7 %copy-start.22 = (s32[4]{0:T(128)S(1)}, s32[4]{0:T(128)}, u32[]{:S(2)}) copy-start(s32[4]{0:T(128)} %param.30) | copy-start | bytes 52
  84.1 11.8 %collective-permute-start = (bf16[2,512,128]{2,1,0:T(8,128)(2,1)S(1)}, bf16[2,512,128]{2,1,0:T(8,128)(2,1)S(1)}, u32[]{:S(2)}, u32[]{:S(2)}) collective-permute-start(bf16[2,512,128]{2,1,0:T(8,128)(2,1)S(1)} %copy.62), channel_id=1, source_target_pairs={{24,0},{0,8},{8,16},{16,24},{25,1},{1,9},{9,17},{17,25},{26,2},{2,... | collective-permute-start | bytes 786440 | tf_op jit(solution)/shard_map/ppermute | solution.py:271
  86.5 19.5 %collective-permute-start.1 = (bf16[2,512,128]{2,1,0:T(8,128)(2,1)S(1)}, bf16[2,512,128]{2,1,0:T(8,128)(2,1)S(1)}, u32[]{:S(2)}, u32[]{:S(2)}) collective-permute-start(bf16[2,512,128]{2,1,0:T(8,128)(2,1)S(1)} %copy.62), channel_id=1, source_target_pairs={{16,0},{24,8},{0,16},{8,24},{17,1},{25,9},{1,17},{9,25},{18,2},{26... | collective-permute-start | bytes 786440 | tf_op jit(solution)/shard_map/ppermute | solution.py:271
  89.1 16.9 %collective-permute-start.2 = (bf16[2,512,128]{2,1,0:T(8,128)(2,1)S(1)}, bf16[2,512,128]{2,1,0:T(8,128)(2,1)S(1)}, u32[]{:S(2)}, u32[]{:S(2)}) collective-permute-start(bf16[2,512,128]{2,1,0:T(8,128)(2,1)S(1)} %copy.62), channel_id=1, source_target_pairs={{8,0},{16,8},{24,16},{0,24},{9,1},{17,9},{25,17},{1,25},{10,2},{18... | collective-permute-start | bytes 786440 | tf_op jit(solution)/shard_map/ppermute | solution.py:271
  92.7 15.2 %copy-start.19 = (f32[1,64]{1,0:T(1,128)S(1)}, f32[1,64]{1,0:T(1,128)}, u32[]{:S(2)}) copy-start(f32[1,64]{1,0:T(1,128)} %param.27) | copy-start | bytes 772
  92.8 15.2 %copy-start.20 = (f32[1,64]{1,0:T(1,128)S(1)}, f32[1,64]{1,0:T(1,128)}, u32[]{:S(2)}) copy-start(f32[1,64]{1,0:T(1,128)} %param.28) | copy-start | bytes 772
  106.8 7.1 %copy-start.12 = (f32[2,512]{1,0:T(2,128)S(1)}, f32[2,512]{1,0:T(2,128)}, u32[]{:S(2)}) copy-start(f32[2,512]{1,0:T(2,128)} %constant.170) | copy-start | bytes 12292
  106.8 7.1 %copy-start.13 = (f32[512]{0:T(512)S(1)}, f32[512]{0:T(512)}, u32[]{:S(2)}) copy-start(f32[512]{0:T(512)} %constant.171) | copy-start | bytes 6148
  106.8 45.3 %all-gather.5.cloned.1.call-start = ((), (), s32[]{:S(2)}) async-start(), calls=%async_computation.2 | async-start | bytes 2621440 | tf_op jit(solution)/shard_map/all_gather | solution.py:276
  164.0 27.5 %copy-start.6 = (bf16[512,1024]{1,0:T(8,128)(2,1)S(1)}, bf16[512,1024]{1,0:T(8,128)(2,1)}, u32[]{:S(2)}) copy-start(bf16[512,1024]{1,0:T(8,128)(2,1)} %pad_maximum_fusion.2) | copy-start | bytes 3145732
  242.5 1.4 copy-start.11
  242.5 1.4 copy-start.18
  248.3 3.3 %copy-start.9 = (bf16[128,128]{1,0:T(8,128)(2,1)S(1)}, bf16[128,128]{1,0:T(8,128)(2,1)}, u32[]{:S(2)}) copy-start(bf16[128,128]{1,0:T(8,128)(2,1)} %constant.152.clone) | copy-start | bytes 98308
  253.7 3.8 %copy-start.23 = (f32[64]{0:T(128)S(1)}, f32[64]{0:T(128)}, u32[]{:S(2)}) copy-start(f32[64]{0:T(128)} %param.29) | copy-start | bytes 772
  253.7 29.4 %all-to-all-start.1 = ((bf16[4,2048,128]{2,1,0:T(8,128)(2,1)}), bf16[4,2048,128]{2,1,0:T(8,128)(2,1)S(1)}, u32[]{:S(2)}, u32[]{:S(2)}) async-start(bf16[4,2048,128]{2,1,0:T(8,128)(2,1)} %bitcast.49), calls=%async_computation.1 | async-start | bytes 4194304 | tf_op jit(solution)/shard_map/all_to_all | solution.py:304
  260.0 23.5 %copy-start.2 = (f32[512,128]{1,0:T(8,128)S(1)}, f32[512,128]{1,0:T(8,128)}, u32[]{:S(2)}) copy-start(f32[512,128]{1,0:T(8,128)} %shard_map.221) | copy-start | bytes 786436
  283.5 13.5 %collective-permute-start.3 = (bf16[2,2,512,128]{3,2,1,0:T(8,128)(2,1)S(1)}, bf16[2,2,512,128]{3,2,1,0:T(8,128)(2,1)S(1)}, u32[]{:S(2)}, u32[]{:S(2)}) collective-permute-start(bf16[2,2,512,128]{3,2,1,0:T(8,128)(2,1)S(1)} %multiply_convert_fusion), channel_id=1, source_target_pairs={{0,1},{1,0},{2,3},{3,2},{4,5},{5,4},{6,7},{7,6},{8,9},{9,8},{10,11... | collective-permute-start | bytes 1572872 | tf_op jit(solution)/shard_map/ppermute | solution.py:309
Sparse Core Ops, SparseCore 0:
  44.8 25.1 all-gather.6
  107.0 20.6 all-gather.8
  129.3 22.8 all-gather.4

commit v2 on v1

--- a/solution.py
+++ b/solution.py
@@ -21,11 +21,12 @@
     return jnp.cos(angle), jnp.sin(angle)
 
 
-def outer_cis(start, count, freqs, npix):
+def outer_cis(start, count, freqs, npix, stride=1):
     low = 32
     freqs = jnp.asarray(freqs, jnp.int32)
-    c1, s1 = cis(start + low * jnp.arange(count // low, dtype=jnp.int32), freqs, npix)
-    c0, s0 = cis(jnp.arange(low, dtype=jnp.int32), freqs, npix)
+    steps = low * stride * jnp.arange(count // low, dtype=jnp.int32)
+    c1, s1 = cis(start + steps, freqs, npix)
+    c0, s0 = cis(stride * jnp.arange(low, dtype=jnp.int32), freqs, npix)
     c1, s1, c0, s0 = lax.optimization_barrier((c1, s1, c0, s0))
     c1, s1, c0, s0 = c1[:, None], s1[:, None], c0[None], s0[None]
     width = freqs.shape[0]
@@ -57,6 +58,80 @@
         ],
         out_specs=[pl.BlockSpec((rows, 128), lambda i: (0, i)) for _ in values],
     )(idx, tab)
+
+
+def forward_kernel(m_ref, mask_ref, f_ref, a_ref, even, odd):
+    half = even.shape[1]
+    cols = a_ref.shape[2] // 2
+    for t in range(mask_ref.shape[0]):
+        rows = pl.ds(t * TILE, TILE)
+        lo = m_ref[rows, :half].astype(F32) * mask_ref[t : t + 1, :half]
+        hi = m_ref[rows, half:].astype(F32) * mask_ref[t : t + 1, half:]
+        even[rows, :] = (lo + hi).astype(BF)
+        odd[rows, :] = (lo - hi).astype(BF)
+    for p, side in enumerate((even, odd)):
+        out = jnp.dot(side[...], f_ref[p], preferred_element_type=F32).astype(BF)
+        for q in range(a_ref.shape[0]):
+            a_ref[q, :, p * cols : (p + 1) * cols] = out[:, q * cols : (q + 1) * cols]
+
+
+def forward(m, mask, table, nrows, cols):
+    height, npix = m.shape
+    return pl.pallas_call(
+        forward_kernel,
+        out_shape=jax.ShapeDtypeStruct((nrows, height, 2 * cols), BF),
+        scratch_shapes=[pltpu.VMEM((height, npix // 2), BF)] * 2,
+        compiler_params=pltpu.CompilerParams(vmem_limit_bytes=VMEM_LIMIT),
+    )(m, mask, table)
+
+
+def sum_kernel(cols, step_size, a_ref, t_ref, lx_ref, perm_ref, out_ref):
+    kf = t_ref.shape[0] // 2
+    shape = (kf, 128)
+    ky = lax.broadcasted_iota(jnp.int32, shape, 0) - kf // 2
+    ly = ky.astype(F32) * step_size
+    first = (lax.broadcasted_iota(jnp.int32, shape, 1) & (cols - 1)) < cols // 2
+    sides = []
+    for p in range(2):
+        lx = lx_ref[p]
+        rhs = jnp.concatenate([a_ref[2 * i + p] for i in range(4)], axis=1)
+        pq = jnp.dot(t_ref[...], rhs, preferred_element_type=F32)
+        pairs = []
+        for pair in range(2):
+            x = pq[:, pair * 128 : (pair + 1) * 128]
+            y = pq[:, (2 + pair) * 128 : (3 + pair) * 128]
+            even = lx * x[:kf] + ly * y[:kf]
+            turned = jnp.where(
+                first,
+                -pltpu.roll(even, 128 - cols // 2, axis=1),
+                pltpu.roll(even, cols // 2, axis=1),
+            )
+            pairs.append((lx * x[kf:] + ly * y[kf:] + turned).astype(BF))
+        sides.append(pairs)
+    for pair in range(2):
+        both = jnp.concatenate([sides[0][pair], sides[1][pair]], axis=1)
+        moved = jnp.dot(both, perm_ref[...], preferred_element_type=F32).astype(BF)
+        out_ref[0, pair, 0] = moved[:, :128]
+        out_ref[0, pair, 1] = moved[:, 128:]
+
+
+def row_sums(a, table, lx, perm, cols, step_size):
+    _, height, wide = a.shape
+    kf = table.shape[0] // 2
+    blocks = wide // 128
+    return pl.pallas_call(
+        functools.partial(sum_kernel, cols, step_size),
+        out_shape=jax.ShapeDtypeStruct((blocks, 2, 2, kf, 128), BF),
+        grid=(blocks,),
+        in_specs=[
+            pl.BlockSpec((8, height, 128), lambda i: (0, 0, i)),
+            pl.BlockSpec(table.shape, lambda i: (0, 0)),
+            pl.BlockSpec((2, 1, 128), lambda i: (0, 0, i)),
+            pl.BlockSpec(perm.shape, lambda i: (0, 0)),
+        ],
+        out_specs=pl.BlockSpec((1, 2, 2, kf, 128), lambda i: (i, 0, 0, 0, 0)),
+        compiler_params=pltpu.CompilerParams(vmem_limit_bytes=VMEM_LIMIT),
+    )(a, table, lx, perm)
 
 
 def ky_kernel(cols, x_ref, w_ref, gx_ref, gy_ref, t_ref, y_ref):
@@ -108,28 +183,28 @@
     )(x, w, gx, gy, table)
 
 
-def pixel_kernel(xt, y_ref, yp_ref, f_ref, a_ref, legs, prods):
+def pixel_kernel(xt, ys_ref, yd_ref, yp_ref, f_ref, a_ref, legs, prods):
     step = pl.program_id(0)
-    height = y_ref.shape[2]
+    height = ys_ref.shape[2]
     wide = f_ref.shape[2]
     here = pl.ds(pl.multiple_of(step * xt, xt), xt)
     dims = (((1,), (1,)), ((), ()))
 
-    def make(source, m, leg, slot):
+    def make(source, leg, slot):
         even = lax.dot_general(
-            source[m, leg, :, :wide], f_ref[0, here, :], dims, preferred_element_type=F32
+            source[0, leg, :, :wide], f_ref[0, here, :], dims, preferred_element_type=F32
         )
         odd = lax.dot_general(
-            source[m, leg, :, wide:], f_ref[1, here, :], dims, preferred_element_type=F32
+            source[0, leg, :, wide:], f_ref[1, here, :], dims, preferred_element_type=F32
         )
         legs[0, slot] = (even + odd).astype(BF)
         legs[1, slot] = (even - odd).astype(BF)
 
     @pl.loop(0, 3)
     def _(leg):
-        make(y_ref, 0, leg, leg)
-        make(y_ref, 1, leg, leg + 3)
-        make(yp_ref, 0, leg, leg + 6)
+        make(ys_ref, leg, leg)
+        make(yd_ref, leg, leg + 3)
+        make(yp_ref, leg, leg + 6)
 
     chunk = 64
 
@@ -158,14 +233,13 @@
         @pl.loop(0, 4)
         def _(i):
             for p in range(2):
-                where = pl.ds(pl.multiple_of(i * (2 * wide) + p * wide, wide), wide)
-                a_ref[:, where] = jnp.dot(
+                a_ref[2 * i + p] = jnp.dot(
                     prods[p, i], f_ref[p], preferred_element_type=F32
                 ).astype(BF)
 
 
-def pixel_products(y, yp, table):
-    height = y.shape[2]
+def pixel_products(ys, yd, yp, table):
+    height = ys.shape[2]
     pixels, wide = table.shape[1:]
     xt = 256
     whole = lambda a: pl.BlockSpec(
@@ -173,16 +247,16 @@
     )
     return pl.pallas_call(
         functools.partial(pixel_kernel, xt),
-        out_shape=jax.ShapeDtypeStruct((height, 8 * wide), BF),
+        out_shape=jax.ShapeDtypeStruct((8, height, wide), BF),
         grid=(pixels // xt,),
-        in_specs=[whole(y), whole(yp), whole(table)],
-        out_specs=pl.BlockSpec((height, 8 * wide), lambda i: (0, 0)),
+        in_specs=[whole(ys), whole(yd), whole(yp), whole(table)],
+        out_specs=pl.BlockSpec((8, height, wide), lambda i: (0, 0, 0)),
         scratch_shapes=[
             pltpu.VMEM((2, 9, height, xt), BF),
             pltpu.VMEM((2, 4, height, pixels), BF),
         ],
         compiler_params=pltpu.CompilerParams(vmem_limit_bytes=VMEM_LIMIT),
-    )(y, yp, table)
+    )(ys, yd, yp, table)
 
 
 def body(nrows, nreal, nfield, sims, data, mask_flags, bins, cl_signal, cl_noise, norm, matching):
@@ -206,18 +280,21 @@
         c, s = outer_cis(0, half, lanes_k[p], npix)
         fx.append((jnp.where(lanes_c[None, :] == 0, c, -s) * forward_scale).astype(BF))
     fx = jnp.stack(fx)
-    c, s = outer_cis(0, npix, ky_order, npix)
-    cs = (jnp.concatenate([c, s], axis=1) * forward_scale).astype(BF)
+    every = np.arange(npix)
+    halves = [outer_cis(p - kf // 2, kh, every, npix, stride=2) for p in range(2)]
+    cs = (
+        jnp.concatenate([halves[0][0], halves[1][0], halves[0][1], halves[1][1]], axis=0)
+        * forward_scale
+    ).astype(BF)
     c, s = outer_cis(row * top, top, ky_order, npix)
     c = (c * forward_scale).astype(BF)
     s = (s * forward_scale).astype(BF)
     gain = jnp.asarray(inverse_gain * inverse_gain, BF)
     t8 = jnp.stack([jnp.concatenate([c[:, :kh], s[:, :kh]], axis=1),
                     jnp.concatenate([c[:, kh:], s[:, kh:]], axis=1)]) * gain
-    c, s = outer_cis(row * top, top, freq, npix)
-    local = (jnp.concatenate([c, s], axis=1) * forward_scale).astype(BF)
-    sign = jnp.asarray(np.tile(1 - 2 * (freq % 2), 2)[None, :], BF)
-    local = jnp.concatenate([local, local * sign], axis=0)
+    near = row * top + jnp.arange(top, dtype=jnp.int32)
+    c, s = outer_cis(-(kf // 2), kf, jnp.concatenate([near, near + half]), npix)
+    local = (jnp.concatenate([c, s], axis=0) * forward_scale).astype(BF)
     fx, cs, t8, local = lax.optimization_barrier((fx, cs, t8, local))
 
     pick = np.zeros((cols, 2, 2, jc), np.float32)
@@ -244,63 +321,47 @@
     flat_bins = bins.reshape(-1, 128)
     ncell = lookup(flat_bins, [norm])[0].reshape(kf, cols)
 
-    mask = jnp.repeat(jnp.repeat(mask_flags, TILE, axis=0), TILE, axis=1) > 0
-    stacked = jnp.concatenate([sims[0], data], axis=0)
-    masked = jnp.where(mask[None], stacked, jnp.zeros_like(stacked))
-    lo, hi = masked[:, :, :half], masked[:, :, half:]
-    flat = lambda a: a.reshape(2 * height, half)
-    parts = [
-        jnp.dot(flat(lo + hi), fx[0], preferred_element_type=F32).astype(BF),
-        jnp.dot(flat(lo - hi), fx[1], preferred_element_type=F32).astype(BF),
-    ]
-    a = jnp.stack([v.reshape(2, height, nrows, cols) for v in parts])
-    a = a.transpose(3, 2, 1, 0, 4).reshape(nrows * height, 4 * cols)
-    a = lax.all_to_all(a, "rows", split_axis=0, concat_axis=0, tiled=True)
-    pq = lax.dot_general(cs, a, (((0,), (0,)), ((), ())), preferred_element_type=F32)
-    pq = pq.reshape(2, kf, 2, 2, 2, jc)
-    x = jnp.stack(
-        [pq[0, ..., 0, :] + pq[1, ..., 1, :], pq[0, ..., 1, :] - pq[1, ..., 0, :]], axis=3
-    )
-    x = x.astype(BF).transpose(1, 2, 0, 3, 4).reshape(2, 2, kf, cols)
+    mask = jnp.repeat(mask_flags.astype(F32), TILE, axis=1)
+
+    def cells_of(m):
+        a = forward(m, mask, fx, nrows, cols).reshape(nrows * height, 2 * cols)
+        a = lax.all_to_all(a, "rows", split_axis=0, concat_axis=0, tiled=True)
+        pq = jnp.dot(cs, a, preferred_element_type=F32).reshape(2, kf, 2, 2, jc)
+        x = jnp.stack(
+            [pq[0, ..., 0, :] + pq[1, ..., 1, :], pq[0, ..., 1, :] - pq[1, ..., 0, :]], axis=2
+        )
+        return x.astype(BF).transpose(1, 0, 2, 3).reshape(2, kf, cols)
+
+    def ky_part(cells):
+        full = lax.all_gather(cells[None], "rows", axis=3, tiled=True)
+        return ky_inverse(full, w, gx, gy, t8, cols)
+
+    x = cells_of(sims[0, 0])
+    xd = cells_of(data[0])
 
     real = lax.axis_index("real")
     ids = jnp.arange(nreal, dtype=jnp.int32)
     partner = jnp.sum(jnp.where(ids == real, matching, 0))
-    px = x[0]
+    px = x
     for shift in range(1, nreal):
         came = lax.ppermute(
-            x[0], "real", [((d + shift) % nreal, d) for d in range(nreal)]
+            x, "real", [((d + shift) % nreal, d) for d in range(nreal)]
         )
         px = jnp.where(lax.rem(real + shift, nreal) == partner, came, px)
 
-    both = lax.all_gather(x, "rows", axis=3, tiled=True)
-    y = ky_inverse(both, w, gx, gy, t8, cols)
-    other = lax.all_gather(px[None], "rows", axis=3, tiled=True)
-    yp = ky_inverse(other, w, gx, gy, t8, cols)
-    field_a = pixel_products(y, yp, fx)
-
-    sums = lax.dot_general(local, field_a, (((0,), (0,)), ((), ())), preferred_element_type=F32)
-    sums = sums.reshape(2, kf, 2, 2, 2, nrows, 2, jc)
-    s_re = sums[0, ..., 0, :] + sums[1, ..., 1, :]
-    s_im = sums[0, ..., 1, :] - sums[1, ..., 0, :]
-    lxo = jnp.asarray(
-        np.stack([freq[p::2] for p in range(2)]).reshape(1, 1, 2, nrows, jc) * step_size, F32
-    )
-    lyo = jnp.asarray(freq.reshape(kf, 1, 1, 1, 1) * step_size, F32)
-    terms = jnp.stack(
-        [
-            -(lxo * s_im[:, 0] + lyo * s_im[:, 1]),
-            lxo * s_re[:, 0] + lyo * s_re[:, 1],
-        ],
-        axis=2,
-    ).astype(BF)
-    terms = terms.transpose(4, 1, 2, 0, 3, 5).reshape(nrows * 4 * kf, cols)
-    order = np.zeros((2, jc, cols), np.float32)
-    for p in range(2):
-        order[p, np.arange(jc), 2 * np.arange(jc) + p] = 1.0
-    terms = jnp.dot(
-        terms, jnp.asarray(order.reshape(cols, cols), BF), preferred_element_type=F32
-    ).astype(BF)
+    ys = ky_part(x)
+    yd = ky_part(xd)
+    yp = ky_part(px)
+    field_a = pixel_products(ys, yd, yp, fx)
+
+    perm = np.zeros((2, 128, 2, 128), np.float32)
+    at = np.arange(128)
+    for p in range(2):
+        perm[p, at, at % cols // jc, at // cols * cols + 2 * (at % jc) + p] = 1.0
+    perm = jnp.asarray(perm.reshape(256, 256), BF)
+    terms = row_sums(field_a, local, lx, perm, cols, step_size)
+    terms = terms.reshape(-1, 2, 2, kf, 128 // cols, cols).transpose(0, 4, 1, 2, 3, 5)
+    terms = terms.reshape(nrows * 4 * kf, cols)
     got = lax.all_to_all(terms, "rows", split_axis=0, concat_axis=0, tiled=True)
     got = jnp.sum(got.reshape(nrows, 2, 2, kf, cols).astype(F32), axis=0)
     mine = (got * ncell).astype(BF)

time: 306 us -> 216 us (0.71)
  local copies, waits for them, and re-layouts: 52.6 us -> 5.43 us
  waiting for transfers between devices: 99.2 us -> 65.9 us
  other arithmetic: 45.4 us -> 23.9 us
  Pallas kernels: 53.5 us -> 72.7 us
  matrix products: 22.6 us -> 7.68 us
  starting transfers between devices: 16.1 us -> 20.7 us
    all_gather x2 -> x3, waiting for transfers between devices: 27.4 us -> 0.01 us  [ky_part(): full = lax.all_gather(cells[None], 'rows', axis=3, tiled=True)]
    reshape x3 -> x1, local copies, waits for them, and re-layouts: 26.3 us -> 0.17 us  [cells_of(): return x.astype(BF).transpose(1, 0, 2, 3).reshape(2, kf, cols)]
    slice x1 -> x0, other arithmetic: 17.9 us -> none  [body(): s_im = sums[0, ..., 1, :] - sums[1, ..., 0, :]]
    pallas_call x0 -> x3, Pallas kernels: none -> 17 us  [the longest x2 8.97 us: forward(): pl.pallas_call(forward_kernel, out_shape=jax.ShapeDtypeStruct((nrows, hei...]
    dot_general x5 -> x2, matrix products: 22.1 us -> 7.13 us  [cells_of(): pq = jnp.dot(cs, a, preferred_element_type=F32).reshape(2, kf, 2, 2, jc)]
    dot_general x2, local copies, waits for them, and re-layouts: 9.45 us -> 1.28 us  [cells_of(): pq = jnp.dot(cs, a, preferred_element_type=F32).reshape(2, kf, 2, 2, jc)]
    all_to_all x1 -> x2, waiting for transfers between devices: 23.3 us -> 17.5 us  [cells_of(): a = lax.all_to_all(a, 'rows', split_axis=0, concat_axis=0, tiled=True)]
    all_to_all x1 -> x2, starting transfers between devices: 4.37 us -> 8.07 us  [cells_of(): a = lax.all_to_all(a, 'rows', split_axis=0, concat_axis=0, tiled=True)]
  transfers between devices with their start and end apart: 9 -> 11, of which waited for: 7 -> 6; matrix products, arithmetic and copies ran while one was open for 8% -> 9% of each run, Pallas kernels for 5% -> 12%
where the time goes in v2:
time: 216 us; the launch traced here: 212 us
  Pallas kernels  72.7 us (34%)
  waiting for transfers between devices  65.9 us (31%)
  other arithmetic  23.9 us (11%)
  starting transfers between devices  20.7 us (10%)
  between operations  15.4 us (7%)
  matrix products  7.68 us (4%)
  local copies, waits for them, and re-layouts  5.43 us (3%)
    pallas_call x1, Pallas kernels, pixel_products(): pl.pallas_call(functools.partial(pixel_kernel, xt), out_shape=jax.ShapeDt...  27.4 us
    all_to_all x1, waiting for transfers between devices, body(): got = lax.all_to_all(terms, 'rows', split_axis=0, concat_axis=0, tiled=True)  23.2 us
    pallas_call x3, Pallas kernels, ky_inverse(): pl.pallas_call(functools.partial(ky_kernel, cols), out_shape=jax.ShapeDty...  21 us
    all_to_all x2, waiting for transfers between devices, cells_of(): a = lax.all_to_all(a, 'rows', split_axis=0, concat_axis=0, tiled=True)  17.5 us
    ppermute x3, waiting for transfers between devices, body(): lax.ppermute(x, 'real', [((d + shift) % nreal, d) for d in range(nreal)])  13.1 us
    ppermute x1, waiting for transfers between devices, body(): lax.ppermute(mine, 'field', [(d, (d + shift) % nfield) for d in range(nfi...  12 us
    pallas_call x2, Pallas kernels, forward(): pl.pallas_call(forward_kernel, out_shape=jax.ShapeDtypeStruct((nrows, hei...  8.97 us
    pallas_call x1, Pallas kernels, row_sums(): pl.pallas_call(functools.partial(sum_kernel, cols, step_size), out_shape=...  8.07 us
  transfers between devices with their start and end apart: 11, of which 6 were waited for; matrix products, arithmetic and copies ran while one was open for 9% of the time, Pallas kernels for 12%

profile of v2, /device:TPU:0, one launch (start us, length us, event | category | flops | bytes accessed | tf_op | source)
XLA Modules:
  0.0 211.8 jit_solution(2880340857349516385)
XLA Ops:
  6.6 1.0 fusion.75
  7.5 0.8 fusion.92
  8.4 0.2 multiply_convert_fusion.2
  8.6 1.8 fusion.83
  10.4 0.3 fusion.79
  10.7 0.2 fusion.90
  10.9 1.1 fusion.24
  12.0 0.3 fusion.73
  12.3 0.3 fusion.71
  12.7 0.9 maximum_multiply_fusion.2.t_ref
  13.6 1.3 multiply_subtract_fusion.2
  14.8 1.2 fusion.5
  16.0 1.5 pad_maximum_fusion.f_ref
  17.5 0.3 multiply_subtract_fusion.4
  17.8 1.3 fusion.1.t_ref
  19.1 0.6 multiply_subtract_fusion.1
  19.7 0.6 multiply_subtract_fusion
  20.3 2.7 %fusion = bf16[1024,2048]{1,0:T(8,128)(2,1)} fusion(f32[256,2048]{1,0:T(8,128)S(1)} %bitcast.141, f32[256,2048]{1,0:T(8,128)S(1)} %bitcast.139, f32[256,2048]{1,0:T(8,128)S(1)} %bitcast.140, f32[256,2048]{1,0:T(8,128)S(1)} %bitcast.138), kind=kLoop, calls=%fused_computation.1 | loop fusion | flops 10485760 | bytes 12582912 | tf_op jit(solution)/shard_map/convert_element_type | solution.py:288
  23.0 0.1 broadcast_bitcast_fusion
  23.1 0.6 copy.54
  23.7 4.5 %shard_map.193 = bf16[4,512,256]{2,1,0:T(8,128)(2,1)} custom-call(bf16[512,2048]{1,0:T(8,128)(2,1)} %bitcast.151, f32[4,2048]{1,0:T(4,128)} %bitcast.162, bf16[2,1024,512]{2,1,0:T(8,128)(2,1)} %pad_maximum_fusion.f_ref), custom_call_target="tpu_custom_call" | custom-call | tf_op jit(solution)/shard_map/pallas_call | solution.py:80
  28.2 4.4 %all-to-all-start.1 = ((bf16[4,512,256]{2,1,0:T(8,128)(2,1)}), bf16[4,512,256]{2,1,0:T(8,128)(2,1)S(1)}, u32[]{:S(2)}, u32[]{:S(2)}) async-start(bf16[4,512,256]{2,1,0:T(8,128)(2,1)} %shard_map.193), calls=%async_computation.1 | async-start | bytes 2097152 | tf_op jit(solution)/shard_map/all_to_all | solution.py:328
  32.6 0.6 convolution_convert_fusion
  33.1 0.8 copy.36
  34.0 4.5 %shard_map.190 = bf16[4,512,256]{2,1,0:T(8,128)(2,1)} custom-call(bf16[512,2048]{1,0:T(8,128)(2,1)} %bitcast.152, f32[4,2048]{1,0:T(4,128)} %bitcast.163, bf16[2,1024,512]{2,1,0:T(8,128)(2,1)} %pad_maximum_fusion.f_ref), custom_call_target="tpu_custom_call" | custom-call | tf_op jit(solution)/shard_map/pallas_call | solution.py:80
  38.5 8.5 %all-to-all-done.1 = bf16[4,512,256]{2,1,0:T(8,128)(2,1)S(1)} async-done(((bf16[4,512,256]{2,1,0:T(8,128)(2,1)}), bf16[4,512,256]{2,1,0:T(8,128)(2,1)S(1)}, u32[]{:S(2)}, u32[]{:S(2)}) %all-to-all-start.1) | async-done | bytes 1048608 | tf_op jit(solution)/shard_map/all_to_all | solution.py:328
  47.0 3.7 %all-to-all-start = ((bf16[4,512,256]{2,1,0:T(8,128)(2,1)}), bf16[4,512,256]{2,1,0:T(8,128)(2,1)S(1)}, u32[]{:S(2)}, u32[]{:S(2)}) async-start(bf16[4,512,256]{2,1,0:T(8,128)(2,1)} %shard_map.190), calls=%async_computation | async-start | bytes 2097152 | tf_op jit(solution)/shard_map/all_to_all | solution.py:328
  50.7 0.0 all-gather.10.cloned.1.call-start
  50.8 0.6 copy.37
  51.4 3.5 %fusion.102 = f32[2,512,2,2,64]{1,4,3,2,0:T(8,128)S(1)} fusion(bf16[2,512,2048,1,1]{2,1,4,3,0:T(8,128)(2,1)} %bitcast.142, bf16[2,2,64,2048,1]{3,2,1,0,4:T(8,128)(2,1)S(1)} %bitcast.156), kind=kOutput, calls=%fused_computation.196 | convolution fusion | flops 1073741824 | bytes 6291456 | tf_op jit(solution)/shard_map/dot_general | solution.py:329
  55.1 0.9 copy.41
  55.9 0.0 all-gather.10.cloned.1.call-update
  55.9 0.0 all-gather.6.cloned.1.call-start
  56.0 9.0 %all-to-all-done = bf16[4,512,256]{2,1,0:T(8,128)(2,1)S(1)} async-done(((bf16[4,512,256]{2,1,0:T(8,128)(2,1)}), bf16[4,512,256]{2,1,0:T(8,128)(2,1)S(1)}, u32[]{:S(2)}, u32[]{:S(2)}) %all-to-all-start) | async-done | bytes 1048608 | tf_op jit(solution)/shard_map/all_to_all | solution.py:328
  65.0 0.6 copy.31
  65.6 3.7 %fusion.101 = f32[2,512,2,2,64]{1,4,3,2,0:T(8,128)S(1)} fusion(bf16[2,512,2048,1,1]{2,1,4,3,0:T(8,128)(2,1)} %bitcast.143, bf16[2,2,64,2048,1]{3,2,1,0,4:T(8,128)(2,1)S(1)} %bitcast.155), kind=kOutput, calls=%fused_computation.195 | convolution fusion | flops 1073741824 | bytes 6291456 | tf_op jit(solution)/shard_map/dot_general | solution.py:329
  69.5 0.8 copy.35
  70.4 0.0 all-gather.12.cloned.1.call-start
  70.4 0.2 copy.43
  70.6 3.3 %collective-permute-start = (bf16[2,512,128]{2,1,0:T(8,128)(2,1)S(1)}, bf16[2,512,128]{2,1,0:T(8,128)(2,1)S(1)}, u32[]{:S(2)}, u32[]{:S(2)}) collective-permute-start(bf16[2,512,128]{2,1,0:T(8,128)(2,1)S(1)} %copy.43), channel_id=1, source_target_pairs={{24,0},{0,8},{8,16},{16,24},{25,1},{1,9},{9,17},{17,25},{26,2},{2,... | collective-permute-start | bytes 786440 | tf_op jit(solution)/shard_map/ppermute | solution.py:347
  73.9 2.8 %collective-permute-start.1 = (bf16[2,512,128]{2,1,0:T(8,128)(2,1)S(1)}, bf16[2,512,128]{2,1,0:T(8,128)(2,1)S(1)}, u32[]{:S(2)}, u32[]{:S(2)}) collective-permute-start(bf16[2,512,128]{2,1,0:T(8,128)(2,1)S(1)} %copy.43), channel_id=1, source_target_pairs={{16,0},{24,8},{0,16},{8,24},{17,1},{25,9},{1,17},{9,25},{18,2},{26... | collective-permute-start | bytes 786440 | tf_op jit(solution)/shard_map/ppermute | solution.py:347
  76.7 1.2 collective-permute-start.2
  77.9 0.7 fusion.94
  80.5 2.9 %collective-permute-done = bf16[2,512,128]{2,1,0:T(8,128)(2,1)S(1)} collective-permute-done((bf16[2,512,128]{2,1,0:T(8,128)(2,1)S(1)}, bf16[2,512,128]{2,1,0:T(8,128)(2,1)S(1)}, u32[]{:S(2)}, u32[]{:S(2)}) %collective-permute-start) | collective-permute-done | bytes 262176 | tf_op jit(solution)/shard_map/ppermute | solution.py:347
  83.4 10.2 %collective-permute-done.1 = bf16[2,512,128]{2,1,0:T(8,128)(2,1)S(1)} collective-permute-done((bf16[2,512,128]{2,1,0:T(8,128)(2,1)S(1)}, bf16[2,512,128]{2,1,0:T(8,128)(2,1)S(1)}, u32[]{:S(2)}, u32[]{:S(2)}) %collective-permute-start.1) | collective-permute-done | bytes 262176 | tf_op jit(solution)/shard_map/ppermute | solution.py:347
  93.6 0.8 select_select_fusion
  94.4 0.0 all-gather.12.cloned.1.call-update
  94.4 0.6 select_maximum_fusion.tab_ref
  95.0 5.4 %shard_map.191 = (f32[1024,512]{1,0:T(8,128)}, f32[1024,512]{1,0:T(8,128)}) custom-call(bf16[1024,512]{1,0:T(8,128)(2,1)} %bitcast.154, f32[8,128]{1,0:T(8,128)} %select_maximum_fusion.tab_ref), custom_call_target="tpu_custom_call" | custom-call | tf_op jit(solution)/shard_map/pallas_call | solution.py:51
  100.4 3.9 %broadcast_multiply_fusion = (f32[2,512,512]{2,1,0:T(8,128)}, f32[2,512,512]{2,1,0:T(8,128)}) fusion(f32[2,512,512]{2,1,0:T(8,128)} %bitcast.150, f32[512]{0:T(512)S(1)} %copy-done.5, f32[2,512]{1,0:T(2,128)S(1)} %copy-done.4), kind=kLoop, calls=%fused_computation.24 | loop fusion | flops 1048576 | bytes 6297600 | tf_op jit(solution)/shard_map/mul | solution.py:320
  104.3 7.1 %shard_map.194.yd_ref = bf16[1,3,512,1024]{3,2,1,0:T(8,128)(2,1)} custom-call(bf16[1,2,512,512]{3,2,1,0:T(8,128)(2,1)} %all-gather.10.cloned.1.call-done.x_ref, f32[2,512,512]{2,1,0:T(8,128)} %bitcast.128, f32[2,512,512]{2,1,0:T(8,128)} %get-tuple-element.68.gx_ref, f32[2,512,512]{2,1,0:T(8,128)} %get-tuple-element.67.gy_ref, ...), custom_call_target="tpu_custom_call" | custom-call | tf_op jit(solution)/shard_map/pallas_call | solution.py:168
  111.4 7.0 %shard_map.192.ys_ref = bf16[1,3,512,1024]{3,2,1,0:T(8,128)(2,1)} custom-call(bf16[1,2,512,512]{3,2,1,0:T(8,128)(2,1)} %all-gather.6.cloned.1.call-done.x_ref, f32[2,512,512]{2,1,0:T(8,128)} %bitcast.129, f32[2,512,512]{2,1,0:T(8,128)} %get-tuple-element.68.gx_ref, f32[2,512,512]{2,1,0:T(8,128)} %get-tuple-element.67.gy_ref, ...), custom_call_target="tpu_custom_call" | custom-call | tf_op jit(solution)/shard_map/pallas_call | solution.py:168
  118.4 6.9 %shard_map.195.yp_ref = bf16[1,3,512,1024]{3,2,1,0:T(8,128)(2,1)} custom-call(bf16[1,2,512,512]{3,2,1,0:T(8,128)(2,1)} %bitcast.161, f32[2,512,512]{2,1,0:T(8,128)} %bitcast.130, f32[2,512,512]{2,1,0:T(8,128)} %get-tuple-element.68.gx_ref, f32[2,512,512]{2,1,0:T(8,128)} %get-tuple-element.67.gy_ref, bf16[2,256,512]{2,1,0:T(8,128)(2,1)} %maximum_multiply_fusion.2.t_ref), custom_call_target="tpu_custom_call" | custom-call | tf_op jit(solution)/shard_map/pallas_call | solution.py:168
  125.3 27.4 %shard_map.196.a_ref = bf16[8,512,512]{2,1,0:T(8,128)(2,1)} custom-call(bf16[1,3,512,1024]{3,2,1,0:T(8,128)(2,1)} %shard_map.192.ys_ref, bf16[1,3,512,1024]{3,2,1,0:T(8,128)(2,1)} %shard_map.194.yd_ref, bf16[1,3,512,1024]{3,2,1,0:T(8,128)(2,1)} %shard_map.195.yp_ref, bf16[2,1024,512]{2,1,0:T(8,128)(2,1)} %pad_maximum_fusion.f_ref), custom_call_target="tpu_custom_call" | custom-call | tf_op jit(solution)/shard_map/pallas_call | solution.py:248
  152.7 8.1 %shard_map.197 = bf16[4,2,2,512,128]{4,3,2,1,0:T(8,128)(2,1)} custom-call(bf16[8,512,512]{2,1,0:T(8,128)(2,1)} %shard_map.196.a_ref, bf16[1024,512]{1,0:T(8,128)(2,1)} %fusion.1.t_ref, f32[2,1,512]{2,1,0:T(1,128)} %constant.164.clone.lx_ref, bf16[256,256]{1,0:T(8,128)(2,1)} %constant.166.clone.perm_ref), custom_call_target="tpu_custom_call" | custom-call | tf_op jit(solution)/shard_map/pallas_call | solution.py:122
  160.8 3.7 %all-to-all-start.2 = ((bf16[4,2048,128]{2,1,0:T(8,128)(2,1)}), bf16[4,2048,128]{2,1,0:T(8,128)(2,1)S(1)}, u32[]{:S(2)}, u32[]{:S(2)}) async-start(bf16[4,2048,128]{2,1,0:T(8,128)(2,1)} %bitcast.133), calls=%async_computation.2 | async-start | bytes 4194304 | tf_op jit(solution)/shard_map/all_to_all | solution.py:365
  164.6 0.6 pad.22.tab_ref
  165.2 1.9 shard_map.198
  167.1 23.2 %all-to-all-done.2 = bf16[4,2048,128]{2,1,0:T(8,128)(2,1)S(1)} async-done(((bf16[4,2048,128]{2,1,0:T(8,128)(2,1)}), bf16[4,2048,128]{2,1,0:T(8,128)(2,1)S(1)}, u32[]{:S(2)}, u32[]{:S(2)}) %all-to-all-start.2) | async-done | bytes 2097184 | tf_op jit(solution)/shard_map/all_to_all | solution.py:365
  190.2 0.3 convert_reduce_fusion
  190.5 0.1 multiply_convert_fusion
  190.6 1.5 collective-permute-start.3
  192.1 12.0 %collective-permute-done.3 = bf16[2,2,512,128]{3,2,1,0:T(8,128)(2,1)S(1)} collective-permute-done((bf16[2,2,512,128]{3,2,1,0:T(8,128)(2,1)S(1)}, bf16[2,2,512,128]{3,2,1,0:T(8,128)(2,1)S(1)}, u32[]{:S(2)}, u32[]{:S(2)}) %collective-permute-start.3) | collective-permute-done | bytes 524320 | tf_op jit(solution)/shard_map/ppermute | solution.py:370
  204.2 1.1 add_bitcast_fusion
  (55 shorter events, 0.5 us)
Async XLA Ops:
  13.6 1.3 copy-start.9
  20.3 2.7 %copy-start.6 = (s32[4,16]{1,0:T(4,128)S(1)}, s32[4,16]{1,0:T(4,128)}, u32[]{:S(2)}) copy-start(s32[4,16]{1,0:T(4,128)} %param.22) | copy-start | bytes 772
  28.2 4.4 %copy-start.1 = (s32[512,128]{1,0:T(8,128)S(1)}, s32[512,128]{1,0:T(8,128)}, u32[]{:S(2)}) copy-start(s32[512,128]{1,0:T(8,128)} %idx_ref.1) | copy-start | bytes 786436
  28.2 4.4 %copy-start.2 = (bf16[512,512]{1,0:T(8,128)(2,1)S(1)}, bf16[512,512]{1,0:T(8,128)(2,1)}, u32[]{:S(2)}) copy-start(bf16[512,512]{1,0:T(8,128)(2,1)} %constant.162.clone) | copy-start | bytes 1572868
  28.2 4.4 %copy-start.3 = (bf16[128,256]{1,0:T(8,128)(2,1)S(1)}, bf16[128,256]{1,0:T(8,128)(2,1)}, u32[]{:S(2)}) copy-start(bf16[128,256]{1,0:T(8,128)(2,1)} %constant.163.clone) | copy-start | bytes 196612
  28.2 18.8 %all-to-all-start.1 = ((bf16[4,512,256]{2,1,0:T(8,128)(2,1)}), bf16[4,512,256]{2,1,0:T(8,128)(2,1)S(1)}, u32[]{:S(2)}, u32[]{:S(2)}) async-start(bf16[4,512,256]{2,1,0:T(8,128)(2,1)} %shard_map.193), calls=%async_computation.1 | async-start | bytes 2097152 | tf_op jit(solution)/shard_map/all_to_all | solution.py:328
  32.6 62.5 %all-gather.8.cloned.1.call-start = ((), (), s32[]{:S(2)}) async-start(), calls=%async_computation.4 | async-start | bytes 1310720 | tf_op jit(solution)/shard_map/all_gather | solution.py:311
  47.0 18.0 %all-to-all-start = ((bf16[4,512,256]{2,1,0:T(8,128)(2,1)}), bf16[4,512,256]{2,1,0:T(8,128)(2,1)S(1)}, u32[]{:S(2)}, u32[]{:S(2)}) async-start(bf16[4,512,256]{2,1,0:T(8,128)(2,1)} %shard_map.190), calls=%async_computation | async-start | bytes 2097152 | tf_op jit(solution)/shard_map/all_to_all | solution.py:328
  50.7 53.6 %all-gather.10.cloned.1.call-start = ((), (), s32[]{:S(2)}) async-start(), calls=%async_computation.5 | async-start | bytes 1310720 | tf_op jit(solution)/shard_map/all_gather | solution.py:336
  55.9 55.4 %all-gather.6.cloned.1.call-start = ((), (), s32[]{:S(2)}) async-start(), calls=%async_computation.3 | async-start | bytes 1310720 | tf_op jit(solution)/shard_map/all_gather | solution.py:336
  69.3 8.6 %copy-start.10 = (s32[4]{0:T(128)S(1)}, s32[4]{0:T(128)}, u32[]{:S(2)}) copy-start(s32[4]{0:T(128)} %param.27) | copy-start | bytes 52
  69.4 25.0 %copy-start.7 = (f32[1,64]{1,0:T(1,128)S(1)}, f32[1,64]{1,0:T(1,128)}, u32[]{:S(2)}) copy-start(f32[1,64]{1,0:T(1,128)} %param.24) | copy-start | bytes 772
  69.4 25.0 %copy-start.8 = (f32[1,64]{1,0:T(1,128)S(1)}, f32[1,64]{1,0:T(1,128)}, u32[]{:S(2)}) copy-start(f32[1,64]{1,0:T(1,128)} %param.25) | copy-start | bytes 772
  69.5 30.9 %copy-start.4 = (f32[2,512]{1,0:T(2,128)S(1)}, f32[2,512]{1,0:T(2,128)}, u32[]{:S(2)}) copy-start(f32[2,512]{1,0:T(2,128)} %constant.182) | copy-start | bytes 12292
  69.5 30.9 %copy-start.5 = (f32[512]{0:T(512)S(1)}, f32[512]{0:T(512)}, u32[]{:S(2)}) copy-start(f32[512]{0:T(512)} %constant.183) | copy-start | bytes 6148
  70.4 48.0 %all-gather.12.cloned.1.call-start = ((), (), s32[]{:S(2)}) async-start(), calls=%async_computation.6 | async-start | bytes 1310720 | tf_op jit(solution)/shard_map/all_gather | solution.py:336
  70.6 12.8 %collective-permute-start = (bf16[2,512,128]{2,1,0:T(8,128)(2,1)S(1)}, bf16[2,512,128]{2,1,0:T(8,128)(2,1)S(1)}, u32[]{:S(2)}, u32[]{:S(2)}) collective-permute-start(bf16[2,512,128]{2,1,0:T(8,128)(2,1)S(1)} %copy.43), channel_id=1, source_target_pairs={{24,0},{0,8},{8,16},{16,24},{25,1},{1,9},{9,17},{17,25},{26,2},{2,... | collective-permute-start | bytes 786440 | tf_op jit(solution)/shard_map/ppermute | solution.py:347
  73.9 19.7 %collective-permute-start.1 = (bf16[2,512,128]{2,1,0:T(8,128)(2,1)S(1)}, bf16[2,512,128]{2,1,0:T(8,128)(2,1)S(1)}, u32[]{:S(2)}, u32[]{:S(2)}) collective-permute-start(bf16[2,512,128]{2,1,0:T(8,128)(2,1)S(1)} %copy.43), channel_id=1, source_target_pairs={{16,0},{24,8},{0,16},{8,24},{17,1},{25,9},{1,17},{9,25},{18,2},{26... | collective-permute-start | bytes 786440 | tf_op jit(solution)/shard_map/ppermute | solution.py:347
  76.7 17.0 %collective-permute-start.2 = (bf16[2,512,128]{2,1,0:T(8,128)(2,1)S(1)}, bf16[2,512,128]{2,1,0:T(8,128)(2,1)S(1)}, u32[]{:S(2)}, u32[]{:S(2)}) collective-permute-start(bf16[2,512,128]{2,1,0:T(8,128)(2,1)S(1)} %copy.43), channel_id=1, source_target_pairs={{8,0},{16,8},{24,16},{0,24},{9,1},{17,9},{25,17},{1,25},{10,2},{18... | collective-permute-start | bytes 786440 | tf_op jit(solution)/shard_map/ppermute | solution.py:347
  160.8 3.8 %copy-start.11 = (f32[64]{0:T(128)S(1)}, f32[64]{0:T(128)}, u32[]{:S(2)}) copy-start(f32[64]{0:T(128)} %param.26) | copy-start | bytes 772
  160.8 29.4 %all-to-all-start.2 = ((bf16[4,2048,128]{2,1,0:T(8,128)(2,1)}), bf16[4,2048,128]{2,1,0:T(8,128)(2,1)S(1)}, u32[]{:S(2)}, u32[]{:S(2)}) async-start(bf16[4,2048,128]{2,1,0:T(8,128)(2,1)} %bitcast.133), calls=%async_computation.2 | async-start | bytes 4194304 | tf_op jit(solution)/shard_map/all_to_all | solution.py:365
  167.1 23.5 %copy-start = (f32[512,128]{1,0:T(8,128)S(1)}, f32[512,128]{1,0:T(8,128)}, u32[]{:S(2)}) copy-start(f32[512,128]{1,0:T(8,128)} %shard_map.198) | copy-start | bytes 786436
  190.6 13.5 %collective-permute-start.3 = (bf16[2,2,512,128]{3,2,1,0:T(8,128)(2,1)S(1)}, bf16[2,2,512,128]{3,2,1,0:T(8,128)(2,1)S(1)}, u32[]{:S(2)}, u32[]{:S(2)}) collective-permute-start(bf16[2,2,512,128]{3,2,1,0:T(8,128)(2,1)S(1)} %multiply_convert_fusion), channel_id=1, source_target_pairs={{0,1},{1,0},{2,3},{3,2},{4,5},{5,4},{6,7},{7,6},{8,9},{9,8},{10,11... | collective-permute-start | bytes 1572872 | tf_op jit(solution)/shard_map/ppermute | solution.py:370
Sparse Core Ops, SparseCore 0:
  34.9 19.2 all-gather.7
  56.1 20.3 all-gather.9
  78.0 16.8 all-gather.5
  96.4 18.7 all-gather.11

commit v3 on v2

--- a/solution.py
+++ b/solution.py
@@ -16,24 +16,21 @@
 
 
 def cis(pixels, freqs, npix):
-    phase = jnp.mod(pixels[:, None] * freqs[None, :], npix)
-    angle = phase.astype(F32) * (2.0 * math.pi / npix)
-    return jnp.cos(angle), jnp.sin(angle)
-
-
-def outer_cis(start, count, freqs, npix, stride=1):
-    low = 32
-    freqs = jnp.asarray(freqs, jnp.int32)
-    steps = low * stride * jnp.arange(count // low, dtype=jnp.int32)
-    c1, s1 = cis(start + steps, freqs, npix)
-    c0, s0 = cis(stride * jnp.arange(low, dtype=jnp.int32), freqs, npix)
-    c1, s1, c0, s0 = lax.optimization_barrier((c1, s1, c0, s0))
-    c1, s1, c0, s0 = c1[:, None], s1[:, None], c0[None], s0[None]
-    width = freqs.shape[0]
-    return (
-        (c1 * c0 - s1 * s0).reshape(count, width),
-        (s1 * c0 + c1 * s0).reshape(count, width),
-    )
+    phase = np.mod(np.asarray(pixels)[..., :, None] * np.asarray(freqs)[..., None, :], npix)
+    angle = phase * (2.0 * math.pi / npix)
+    return np.cos(angle).astype(np.float32), np.sin(angle).astype(np.float32)
+
+
+def product_table(high, low):
+    c1, s1 = (jnp.asarray(v)[:, None] for v in high)
+    c0, s0 = (jnp.asarray(v)[None] for v in low)
+    shape = (c1.shape[0] * c0.shape[1], c0.shape[2])
+    return (c1 * c0 - s1 * s0).reshape(shape), (s1 * c0 + c1 * s0).reshape(shape)
+
+
+def outer_cis(start, count, freqs, npix, stride=1, low=32):
+    high = start + low * stride * np.arange(count // low)
+    return product_table(cis(high, freqs, npix), cis(stride * np.arange(low), freqs, npix))
 
 
 def lookup_kernel(idx_ref, tab_ref, *outs):
@@ -57,6 +54,9 @@
             pl.BlockSpec((8, 128), lambda i: (0, 0)),
         ],
         out_specs=[pl.BlockSpec((rows, 128), lambda i: (0, i)) for _ in values],
+        cost_estimate=pl.CostEstimate(
+            flops=rows * width, bytes_accessed=16 * rows * width, transcendentals=0
+        ),
     )(idx, tab)
 
 
@@ -82,6 +82,11 @@
         out_shape=jax.ShapeDtypeStruct((nrows, height, 2 * cols), BF),
         scratch_shapes=[pltpu.VMEM((height, npix // 2), BF)] * 2,
         compiler_params=pltpu.CompilerParams(vmem_limit_bytes=VMEM_LIMIT),
+        cost_estimate=pl.CostEstimate(
+            flops=4 * height * npix * nrows * cols,
+            bytes_accessed=4 * height * npix,
+            transcendentals=0,
+        ),
     )(m, mask, table)
 
 
@@ -94,25 +99,20 @@
     sides = []
     for p in range(2):
         lx = lx_ref[p]
-        rhs = jnp.concatenate([a_ref[2 * i + p] for i in range(4)], axis=1)
+        rhs = jnp.concatenate([a_ref[2 * i + p] for i in range(2)], axis=1)
         pq = jnp.dot(t_ref[...], rhs, preferred_element_type=F32)
-        pairs = []
-        for pair in range(2):
-            x = pq[:, pair * 128 : (pair + 1) * 128]
-            y = pq[:, (2 + pair) * 128 : (3 + pair) * 128]
-            even = lx * x[:kf] + ly * y[:kf]
-            turned = jnp.where(
-                first,
-                -pltpu.roll(even, 128 - cols // 2, axis=1),
-                pltpu.roll(even, cols // 2, axis=1),
-            )
-            pairs.append((lx * x[kf:] + ly * y[kf:] + turned).astype(BF))
-        sides.append(pairs)
-    for pair in range(2):
-        both = jnp.concatenate([sides[0][pair], sides[1][pair]], axis=1)
-        moved = jnp.dot(both, perm_ref[...], preferred_element_type=F32).astype(BF)
-        out_ref[0, pair, 0] = moved[:, :128]
-        out_ref[0, pair, 1] = moved[:, 128:]
+        x, y = pq[:, :128], pq[:, 128:]
+        even = lx * x[:kf] + ly * y[:kf]
+        turned = jnp.where(
+            first,
+            -pltpu.roll(even, 128 - cols // 2, axis=1),
+            pltpu.roll(even, cols // 2, axis=1),
+        )
+        sides.append((lx * x[kf:] + ly * y[kf:] + turned).astype(BF))
+    both = jnp.concatenate(sides, axis=1)
+    moved = jnp.dot(both, perm_ref[...], preferred_element_type=F32).astype(BF)
+    out_ref[0, 0] = moved[:, :128]
+    out_ref[0, 1] = moved[:, 128:]
 
 
 def row_sums(a, table, lx, perm, cols, step_size):
@@ -121,16 +121,19 @@
     blocks = wide // 128
     return pl.pallas_call(
         functools.partial(sum_kernel, cols, step_size),
-        out_shape=jax.ShapeDtypeStruct((blocks, 2, 2, kf, 128), BF),
+        out_shape=jax.ShapeDtypeStruct((blocks, 2, kf, 128), BF),
         grid=(blocks,),
         in_specs=[
-            pl.BlockSpec((8, height, 128), lambda i: (0, 0, i)),
+            pl.BlockSpec((4, height, 128), lambda i: (0, 0, i)),
             pl.BlockSpec(table.shape, lambda i: (0, 0)),
             pl.BlockSpec((2, 1, 128), lambda i: (0, 0, i)),
             pl.BlockSpec(perm.shape, lambda i: (0, 0)),
         ],
-        out_specs=pl.BlockSpec((1, 2, 2, kf, 128), lambda i: (i, 0, 0, 0, 0)),
+        out_specs=pl.BlockSpec((1, 2, kf, 128), lambda i: (i, 0, 0, 0)),
         compiler_params=pltpu.CompilerParams(vmem_limit_bytes=VMEM_LIMIT),
+        cost_estimate=pl.CostEstimate(
+            flops=2 * height * 2 * kf * 4 * wide, bytes_accessed=12 * wide * kf, transcendentals=0
+        ),
     )(a, table, lx, perm)
 
 
@@ -180,32 +183,34 @@
             (1, 3, 2 * top, lanes), lambda p, i, m: (m, 0, 0, p * blocks + i)
         ),
         compiler_params=pltpu.CompilerParams(vmem_limit_bytes=VMEM_LIMIT),
+        cost_estimate=pl.CostEstimate(
+            flops=3 * 16 * maps * top * kf * wide,
+            bytes_accessed=48 * kf * wide,
+            transcendentals=0,
+        ),
     )(x, w, gx, gy, table)
 
 
-def pixel_kernel(xt, ys_ref, yd_ref, yp_ref, f_ref, a_ref, legs, prods):
-    step = pl.program_id(0)
-    height = ys_ref.shape[2]
+DIMS = (((1,), (1,)), ((), ()))
+
+
+def make_legs(source, f_ref, here, dest):
     wide = f_ref.shape[2]
-    here = pl.ds(pl.multiple_of(step * xt, xt), xt)
-    dims = (((1,), (1,)), ((), ()))
-
-    def make(source, leg, slot):
-        even = lax.dot_general(
-            source[0, leg, :, :wide], f_ref[0, here, :], dims, preferred_element_type=F32
-        )
-        odd = lax.dot_general(
-            source[0, leg, :, wide:], f_ref[1, here, :], dims, preferred_element_type=F32
-        )
-        legs[0, slot] = (even + odd).astype(BF)
-        legs[1, slot] = (even - odd).astype(BF)
 
     @pl.loop(0, 3)
     def _(leg):
-        make(ys_ref, leg, leg)
-        make(yd_ref, leg, leg + 3)
-        make(yp_ref, leg, leg + 6)
-
+        even = lax.dot_general(
+            source[0, leg, :, :wide], f_ref[0, here, :], DIMS, preferred_element_type=F32
+        )
+        odd = lax.dot_general(
+            source[0, leg, :, wide:], f_ref[1, here, :], DIMS, preferred_element_type=F32
+        )
+        dest[0, leg] = (even + odd).astype(BF)
+        dest[1, leg] = (even - odd).astype(BF)
+
+
+def make_products(own_ref, other_ref, prods, here):
+    height = own_ref.shape[2]
     chunk = 64
 
     @pl.loop(0, height // chunk)
@@ -213,24 +218,18 @@
         rows = pl.ds(pl.multiple_of(c * chunk, chunk), chunk)
         sides = []
         for side in range(2):
-            own = [legs[side, i, rows, :].astype(F32) for i in range(3)]
-            dat = [legs[side, i + 3, rows, :].astype(F32) for i in range(3)]
-            par = [legs[side, i + 6, rows, :].astype(F32) for i in range(3)]
-            sides.append(
-                (
-                    dat[1] * own[0] + own[1] * dat[0],
-                    own[1] * par[0] + par[1] * own[0],
-                    dat[2] * own[0] + own[2] * dat[0],
-                    own[2] * par[0] + par[2] * own[0],
-                )
-            )
-        for i in range(4):
+            own = [own_ref[side, i, rows, :].astype(F32) for i in range(3)]
+            other = [other_ref[side, i, rows, :].astype(F32) for i in range(3)]
+            sides.append([other[d] * own[0] + own[d] * other[0] for d in (1, 2)])
+        for i in range(2):
             prods[0, i, rows, here] = (sides[0][i] + sides[1][i]).astype(BF)
             prods[1, i, rows, here] = (sides[0][i] - sides[1][i]).astype(BF)
 
-    @pl.when(step == pl.num_programs(0) - 1)
+
+def transform_products(prods, f_ref, a_ref):
+    @pl.when(pl.program_id(0) == pl.num_programs(0) - 1)
     def _():
-        @pl.loop(0, 4)
+        @pl.loop(0, 2)
         def _(i):
             for p in range(2):
                 a_ref[2 * i + p] = jnp.dot(
@@ -238,25 +237,61 @@
                 ).astype(BF)
 
 
-def pixel_products(ys, yd, yp, table):
-    height = ys.shape[2]
+def first_kernel(xt, ys_ref, yd_ref, f_ref, a_ref, own_ref, other, prods):
+    here = pl.ds(pl.multiple_of(pl.program_id(0) * xt, xt), xt)
+    make_legs(ys_ref, f_ref, here, own_ref)
+    make_legs(yd_ref, f_ref, here, other)
+    make_products(own_ref, other, prods, here)
+    transform_products(prods, f_ref, a_ref)
+
+
+def second_kernel(xt, yp_ref, own_ref, f_ref, a_ref, other, prods):
+    here = pl.ds(pl.multiple_of(pl.program_id(0) * xt, xt), xt)
+    make_legs(yp_ref, f_ref, here, other)
+    make_products(own_ref, other, prods, here)
+    transform_products(prods, f_ref, a_ref)
+
+
+def pixel_products(own, other, table, first):
+    height = other.shape[2]
     pixels, wide = table.shape[1:]
     xt = 256
     whole = lambda a: pl.BlockSpec(
         a.shape, lambda i: (0,) * a.ndim, pipeline_mode=pl.Buffered(1)
     )
-    return pl.pallas_call(
-        functools.partial(pixel_kernel, xt),
-        out_shape=jax.ShapeDtypeStruct((8, height, wide), BF),
+    legs_spec = pl.BlockSpec((2, 3, height, xt), lambda i: (0, 0, 0, i))
+    a_shape = jax.ShapeDtypeStruct((4, height, wide), BF)
+    a_spec = pl.BlockSpec((4, height, wide), lambda i: (0, 0, 0))
+    maps = 2 if first else 1
+    params = dict(
         grid=(pixels // xt,),
-        in_specs=[whole(ys), whole(yd), whole(yp), whole(table)],
-        out_specs=pl.BlockSpec((8, height, wide), lambda i: (0, 0, 0)),
         scratch_shapes=[
-            pltpu.VMEM((2, 9, height, xt), BF),
-            pltpu.VMEM((2, 4, height, pixels), BF),
+            pltpu.VMEM((2, 3, height, xt), BF),
+            pltpu.VMEM((2, 2, height, pixels), BF),
         ],
         compiler_params=pltpu.CompilerParams(vmem_limit_bytes=VMEM_LIMIT),
-    )(ys, yd, yp, table)
+        cost_estimate=pl.CostEstimate(
+            flops=2 * height * pixels * wide * (6 * maps + 4),
+            bytes_accessed=2 * height * pixels * 12,
+            transcendentals=0,
+        ),
+    )
+    if first:
+        legs_shape = jax.ShapeDtypeStruct((2, 3, height, pixels), BF)
+        return pl.pallas_call(
+            functools.partial(first_kernel, xt),
+            out_shape=[a_shape, legs_shape],
+            in_specs=[whole(own), whole(other), whole(table)],
+            out_specs=[a_spec, legs_spec],
+            **params,
+        )(own, other, table)
+    return pl.pallas_call(
+        functools.partial(second_kernel, xt),
+        out_shape=a_shape,
+        in_specs=[whole(other), legs_spec, whole(table)],
+        out_specs=a_spec,
+        **params,
+    )(other, own, table)
 
 
 def body(nrows, nreal, nfield, sims, data, mask_flags, bins, cl_signal, cl_noise, norm, matching):
@@ -286,16 +321,35 @@
         jnp.concatenate([halves[0][0], halves[1][0], halves[0][1], halves[1][1]], axis=0)
         * forward_scale
     ).astype(BF)
-    c, s = outer_cis(row * top, top, ky_order, npix)
+    low = 32
+    starts = np.arange(nrows)[:, None] * top + low * np.arange(top // low)
+    high = [
+        lax.dynamic_index_in_dim(jnp.asarray(v), row, keepdims=False)
+        for v in cis(starts, ky_order, npix)
+    ]
+    c, s = product_table(high, cis(np.arange(low), ky_order, npix))
     c = (c * forward_scale).astype(BF)
     s = (s * forward_scale).astype(BF)
     gain = jnp.asarray(inverse_gain * inverse_gain, BF)
     t8 = jnp.stack([jnp.concatenate([c[:, :kh], s[:, :kh]], axis=1),
                     jnp.concatenate([c[:, kh:], s[:, kh:]], axis=1)]) * gain
-    near = row * top + jnp.arange(top, dtype=jnp.int32)
-    c, s = outer_cis(-(kf // 2), kf, jnp.concatenate([near, near + half]), npix)
+    near = np.arange(nrows)[:, None] * top + np.arange(top)
+    near = np.concatenate([near, near + half], axis=1)
+    pieces = []
+    for ks in (low * np.arange(kf // low) - kf // 2, np.arange(low)):
+        ks = np.broadcast_to(ks, (nrows, ks.shape[0]))
+        pieces.append(
+            [
+                lax.dynamic_index_in_dim(jnp.asarray(v), row, keepdims=False)
+                for v in cis(ks, near, npix)
+            ]
+        )
+    c, s = product_table(*pieces)
     local = (jnp.concatenate([c, s], axis=0) * forward_scale).astype(BF)
-    fx, cs, t8, local = lax.optimization_barrier((fx, cs, t8, local))
+    fx = lax.optimization_barrier(fx)
+    cs = lax.optimization_barrier(cs)
+    t8 = lax.optimization_barrier(t8)
+    local = lax.optimization_barrier(local)
 
     pick = np.zeros((cols, 2, 2, jc), np.float32)
     for p in range(2):
@@ -323,9 +377,11 @@
 
     mask = jnp.repeat(mask_flags.astype(F32), TILE, axis=1)
 
-    def cells_of(m):
-        a = forward(m, mask, fx, nrows, cols).reshape(nrows * height, 2 * cols)
-        a = lax.all_to_all(a, "rows", split_axis=0, concat_axis=0, tiled=True)
+    def exchange(a):
+        a = a.reshape(nrows * height, 2 * cols)
+        return lax.all_to_all(a, "rows", split_axis=0, concat_axis=0, tiled=True)
+
+    def cells_of(a):
         pq = jnp.dot(cs, a, preferred_element_type=F32).reshape(2, kf, 2, 2, jc)
         x = jnp.stack(
             [pq[0, ..., 0, :] + pq[1, ..., 1, :], pq[0, ..., 1, :] - pq[1, ..., 0, :]], axis=2
@@ -336,8 +392,13 @@
         full = lax.all_gather(cells[None], "rows", axis=3, tiled=True)
         return ky_inverse(full, w, gx, gy, t8, cols)
 
-    x = cells_of(sims[0, 0])
-    xd = cells_of(data[0])
+    own_a = forward(sims[0, 0], mask, fx, nrows, cols)
+    own_a, second = lax.optimization_barrier((own_a, data[0]))
+    data_a = forward(second, mask, fx, nrows, cols)
+    own_a, w, gx, gy, cs = lax.optimization_barrier((exchange(own_a), w, gx, gy, cs))
+    own_a, data_a = lax.optimization_barrier((own_a, data_a))
+    x = cells_of(own_a)
+    xd = cells_of(exchange(data_a))
 
     real = lax.axis_index("real")
     ids = jnp.arange(nreal, dtype=jnp.int32)
@@ -352,26 +413,40 @@
     ys = ky_part(x)
     yd = ky_part(xd)
     yp = ky_part(px)
-    field_a = pixel_products(ys, yd, yp, fx)
+    first_a, own_legs = pixel_products(ys, yd, fx, True)
 
     perm = np.zeros((2, 128, 2, 128), np.float32)
     at = np.arange(128)
     for p in range(2):
         perm[p, at, at % cols // jc, at // cols * cols + 2 * (at % jc) + p] = 1.0
     perm = jnp.asarray(perm.reshape(256, 256), BF)
-    terms = row_sums(field_a, local, lx, perm, cols, step_size)
-    terms = terms.reshape(-1, 2, 2, kf, 128 // cols, cols).transpose(0, 4, 1, 2, 3, 5)
-    terms = terms.reshape(nrows * 4 * kf, cols)
-    got = lax.all_to_all(terms, "rows", split_axis=0, concat_axis=0, tiled=True)
-    got = jnp.sum(got.reshape(nrows, 2, 2, kf, cols).astype(F32), axis=0)
-    mine = (got * ncell).astype(BF)
-    total = mine.astype(F32)
-    for shift in range(1, nfield):
-        theirs = lax.ppermute(
-            mine, "field", [(d, (d + shift) % nfield) for d in range(nfield)]
-        )
-        total = total + theirs.astype(F32)
-    return total[None]
+
+    def partial_sums(field_a):
+        terms = row_sums(field_a, local, lx, perm, cols, step_size)
+        terms = terms.reshape(-1, 2, kf, 128 // cols, cols).transpose(0, 3, 1, 2, 4)
+        return terms.reshape(nrows * 2 * kf, cols)
+
+    def over_rows(terms):
+        got = lax.all_to_all(terms, "rows", split_axis=0, concat_axis=0, tiled=True)
+        got = jnp.sum(got.reshape(nrows, 2, kf, cols).astype(F32), axis=0)
+        return (got * ncell).astype(BF)
+
+    def over_field(mine):
+        total = mine.astype(F32)
+        for shift in range(1, nfield):
+            theirs = lax.ppermute(
+                mine, "field", [(d, (d + shift) % nfield) for d in range(nfield)]
+            )
+            total = total + theirs.astype(F32)
+        return total
+
+    terms = partial_sums(first_a)
+    terms, own_legs, yp = lax.optimization_barrier((terms, own_legs, yp))
+    mine = over_rows(terms)
+    second_terms = partial_sums(pixel_products(own_legs, yp, fx, False))
+    mine, second_terms = lax.optimization_barrier((mine, second_terms))
+    second_mine = over_rows(second_terms)
+    return jnp.stack([over_field(mine), over_field(second_mine)])[None]
 
 
 def solution(mesh):

time: 216 us -> 218 us (level); the launches traced: 212 us -> 217 us
  Pallas kernels: 72.7 us -> 85.7 us
  waiting for transfers between devices: 65.9 us -> 56 us
  other arithmetic: 23.9 us -> 19.6 us
  starting transfers between devices: 20.7 us -> 24.7 us
  local copies, waits for them, and re-layouts: 5.43 us -> 8.18 us
    all_to_all x3 -> x4, waiting for transfers between devices: 40.7 us -> 16.3 us  [the longest x2 12.9 us: over_rows(): got = lax.all_to_all(terms, 'rows', split_axis=0, concat_axis=0, tiled=True)]
    all_gather x3, waiting for transfers between devices: 0.01 us -> 12.5 us  [ky_part(): full = lax.all_gather(cells[None], 'rows', axis=3, tiled=True)]
    all_gather x1, waiting for transfers between devices: 0.01 us -> 11.1 us  [body(): cells = lax.all_gather(moved, 'rows', axis=2, tiled=True)]
    pallas_call x1 -> x2, Pallas kernels: 27.4 us -> 36.5 us  [the longest x1 21.6 us: pixel_products(): pl.pallas_call(functools.partial(first_kernel, xt), out_shape=[a_shape, l...]
    sin x8 -> x0, other arithmetic: 5.81 us -> none  [cis(): return (jnp.cos(angle), jnp.sin(angle))]
    ppermute x1 -> x2, waiting for transfers between devices: 12 us -> 6.32 us  [over_field(): lax.ppermute(mine, 'field', [(d, (d + shift) % nfield) for d in range(nfi...]
    pallas_call x1 -> x2, Pallas kernels: 8.07 us -> 12.3 us  [row_sums(): pl.pallas_call(functools.partial(sum_kernel, cols, step_size), out_shape=...]
    ppermute x3, waiting for transfers between devices: 13.1 us -> 9.64 us  [body(): lax.ppermute(x, 'real', [((d + shift) % nreal, d) for d in range(nreal)])]
  transfers between devices with their start and end apart: 11 -> 13, of which waited for: 6 -> 7; matrix products, arithmetic and copies ran while one was open for 9% -> 10% of each run, Pallas kernels for 12% -> 21%
where the time goes in v3:
time: 218 us; the launch traced here: 217 us
  Pallas kernels  85.7 us (39%)
  waiting for transfers between devices  56 us (26%)
  starting transfers between devices  24.7 us (11%)
  other arithmetic  19.6 us (9%)
  between operations  15.5 us (7%)
  local copies, waits for them, and re-layouts  8.18 us (4%)
  matrix products  7.5 us (3%)
    pallas_call x1, Pallas kernels, pixel_products(): pl.pallas_call(functools.partial(first_kernel, xt), out_shape=[a_shape, l...  21.6 us
    pallas_call x3, Pallas kernels, ky_inverse(): pl.pallas_call(functools.partial(ky_kernel, cols), out_shape=jax.ShapeDty...  20.7 us
    pallas_call x1, Pallas kernels, pixel_products(): pl.pallas_call(functools.partial(second_kernel, xt), out_shape=a_shape, i...  14.9 us
    all_to_all x2, waiting for transfers between devices, over_rows(): got = lax.all_to_all(terms, 'rows', split_axis=0, concat_axis=0, tiled=True)  12.9 us
    all_gather x3, waiting for transfers between devices, ky_part(): full = lax.all_gather(cells[None], 'rows', axis=3, tiled=True)  12.5 us
    pallas_call x2, Pallas kernels, row_sums(): pl.pallas_call(functools.partial(sum_kernel, cols, step_size), out_shape=...  12.3 us
    all_gather x1, waiting for transfers between devices, body(): cells = lax.all_gather(moved, 'rows', axis=2, tiled=True)  11.1 us
    ppermute x3, waiting for transfers between devices, body(): lax.ppermute(x, 'real', [((d + shift) % nreal, d) for d in range(nreal)])  9.64 us
  transfers between devices with their start and end apart: 13, of which 7 were waited for; matrix products, arithmetic and copies ran while one was open for 10% of the time, Pallas kernels for 21%

profile of v3, /device:TPU:0, one launch (start us, length us, event | category | flops | bytes accessed | tf_op | source)
XLA Modules:
  0.0 217.2 jit_solution(10750136880394715606)
XLA Ops:
  6.5 2.3 %multiply_subtract_fusion.2 = (f32[32,32,512]{2,1,0:T(8,128)S(1)}, f32[32,32,512]{2,1,0:T(8,128)S(1)}, f32[32,32,512]{2,1,0:T(8,128)S(1)}, f32[32,32,512]{2,1,0:T(8,128)S(1)}) fusion(f32[32,512]{1,0:T(8,128)} %constant.118.clone, f32[32,512]{1,0:T(8,128)} %constant.116.clone, f32[32,512]{1,0:T(8,128)} %constant.117.clone, f32[32,512]{1,0:T(8,128)} %constant.115.clone, ...), kind=kLoop, calls=%fused_computation.18 | loop fusion | flops 7340032 | bytes 8912896 | tf_op jit(solution)/shard_map/sub | solution.py:28
  8.9 1.2 fusion.5
  10.1 1.5 pad_maximum_fusion.f_ref
  11.6 0.1 broadcast_bitcast_fusion
  11.7 0.6 copy.73
  12.3 4.5 %shard_map.361 = bf16[4,512,256]{2,1,0:T(8,128)(2,1)} custom-call(bf16[512,2048]{1,0:T(8,128)(2,1)} %bitcast.165, f32[4,2048]{1,0:T(4,128)} %bitcast.163, bf16[2,1024,512]{2,1,0:T(8,128)(2,1)} %pad_maximum_fusion.f_ref), custom_call_target="tpu_custom_call" | custom-call | flops 2147483648 | bytes 4194304 | tf_op jit(solution)/shard_map/pallas_call | solution.py:80
  16.8 4.4 %all-to-all-start = ((bf16[4,512,256]{2,1,0:T(8,128)(2,1)}), bf16[4,512,256]{2,1,0:T(8,128)(2,1)S(1)}, u32[]{:S(2)}, u32[]{:S(2)}) async-start(bf16[4,512,256]{2,1,0:T(8,128)(2,1)} %shard_map.361), calls=%async_computation | async-start | bytes 2097152 | tf_op jit(solution)/shard_map/all_to_all | solution.py:382
  21.2 0.6 convolution_convert_fusion
  21.8 0.9 copy.49
  22.7 0.0 all-gather.8.cloned.1.call-start
  22.8 1.2 multiply_subtract_fusion.1
  24.0 2.7 %fusion = bf16[1024,2048]{1,0:T(8,128)(2,1)} fusion(f32[256,2048]{1,0:T(8,128)S(1)} %bitcast.140, f32[256,2048]{1,0:T(8,128)S(1)} %bitcast.139, f32[256,2048]{1,0:T(8,128)S(1)} %bitcast.141, f32[256,2048]{1,0:T(8,128)S(1)} %bitcast.138), kind=kLoop, calls=%fused_computation.1 | loop fusion | flops 10485760 | bytes 12582912 | tf_op jit(solution)/shard_map/convert_element_type | solution.py:323
  26.7 0.6 select_maximum_fusion.tab_ref
  27.3 4.5 %shard_map.363 = bf16[4,512,256]{2,1,0:T(8,128)(2,1)} custom-call(bf16[512,2048]{1,0:T(8,128)(2,1)} %bitcast.166, f32[4,2048]{1,0:T(4,128)} %bitcast.164, bf16[2,1024,512]{2,1,0:T(8,128)(2,1)} %pad_maximum_fusion.f_ref), custom_call_target="tpu_custom_call" | custom-call | flops 2147483648 | bytes 4194304 | tf_op jit(solution)/shard_map/pallas_call | solution.py:80
  31.8 11.1 %all-gather.6.cloned.1.call-done = bf16[2,512,512]{2,1,0:T(8,128)(2,1)} async-done(((bf16[2,512,128]{2,1,0:T(8,128)(2,1)}), bf16[2,512,512]{2,1,0:T(8,128)(2,1)}) %all-gather.6.cloned.1.call-update) | async-done | bytes 1048592 | tf_op jit(solution)/shard_map/all_gather | solution.py:365
  42.9 5.3 %shard_map.362 = (f32[1024,512]{1,0:T(8,128)}, f32[1024,512]{1,0:T(8,128)}) custom-call(bf16[1024,512]{1,0:T(8,128)(2,1)} %bitcast.154, f32[8,128]{1,0:T(8,128)} %select_maximum_fusion.tab_ref), custom_call_target="tpu_custom_call" | custom-call | flops 524288 | bytes 8388608 | tf_op jit(solution)/shard_map/pallas_call | solution.py:48
  48.3 3.9 %broadcast_multiply_fusion = (f32[2,512,512]{2,1,0:T(8,128)}, f32[2,512,512]{2,1,0:T(8,128)}) fusion(f32[2,512,512]{2,1,0:T(8,128)} %bitcast.150, f32[512]{0:T(512)S(1)} %copy-done.13, f32[2,512]{1,0:T(2,128)S(1)} %copy-done.12), kind=kLoop, calls=%fused_computation.26 | loop fusion | flops 1048576 | bytes 6297600 | tf_op jit(solution)/shard_map/mul | solution.py:374
  52.2 3.5 %fusion.20 = f32[1024,256]{0,1:T(8,128)S(1)} fusion(bf16[1024,2048]{1,0:T(8,128)(2,1)} %fusion, bf16[2048,256]{1,0:T(8,128)(2,1)S(1)} %bitcast.153), kind=kOutput, calls=%fused_computation.75 | convolution fusion | flops 1073741824 | bytes 6291456 | tf_op jit(solution)/shard_map/dot_general | solution.py:385
  55.7 0.9 reshape.474
  56.6 0.6 fusion.10
  57.3 0.8 copy.51
  58.2 0.7 dynamic-slice_bitcast_fusion.4
  58.9 0.2 copy.57
  59.1 2.3 %collective-permute-start = (bf16[2,512,128]{2,1,0:T(8,128)(2,1)S(1)}, bf16[2,512,128]{2,1,0:T(8,128)(2,1)S(1)}, u32[]{:S(2)}, u32[]{:S(2)}) collective-permute-start(bf16[2,512,128]{2,1,0:T(8,128)(2,1)S(1)} %copy.57), channel_id=1, source_target_pairs={{24,0},{0,8},{8,16},{16,24},{25,1},{1,9},{9,17},{17,25},{26,2},{2,... | collective-permute-start | bytes 786440 | tf_op jit(solution)/shard_map/ppermute | solution.py:408
  61.4 2.6 %collective-permute-start.1 = (bf16[2,512,128]{2,1,0:T(8,128)(2,1)S(1)}, bf16[2,512,128]{2,1,0:T(8,128)(2,1)S(1)}, u32[]{:S(2)}, u32[]{:S(2)}) collective-permute-start(bf16[2,512,128]{2,1,0:T(8,128)(2,1)S(1)} %copy.57), channel_id=1, source_target_pairs={{16,0},{24,8},{0,16},{8,24},{17,1},{25,9},{1,17},{9,25},{18,2},{26... | collective-permute-start | bytes 786440 | tf_op jit(solution)/shard_map/ppermute | solution.py:408
  64.0 1.4 collective-permute-start.2
  65.4 0.2 multiply_convert_fusion.3
  65.5 3.7 %all-to-all-start.1 = ((bf16[4,512,256]{2,1,0:T(8,128)(2,1)}), bf16[4,512,256]{2,1,0:T(8,128)(2,1)S(1)}, u32[]{:S(2)}, u32[]{:S(2)}) async-start(bf16[4,512,256]{2,1,0:T(8,128)(2,1)} %shard_map.363), calls=%async_computation.1 | async-start | bytes 2097152 | tf_op jit(solution)/shard_map/all_to_all | solution.py:382
  69.2 0.0 all-gather.12.cloned.1.call-start
  69.3 0.6 fusion.15
  71.9 9.6 %collective-permute-done.1 = bf16[2,512,128]{2,1,0:T(8,128)(2,1)S(1)} collective-permute-done((bf16[2,512,128]{2,1,0:T(8,128)(2,1)S(1)}, bf16[2,512,128]{2,1,0:T(8,128)(2,1)S(1)}, u32[]{:S(2)}, u32[]{:S(2)}) %collective-permute-start.1) | collective-permute-done | bytes 262176 | tf_op jit(solution)/shard_map/ppermute | solution.py:408
  81.5 0.7 select_select_fusion
  82.3 0.0 all-gather.10.cloned.1.call-start
  82.4 3.4 %all-to-all-done.1 = bf16[4,512,256]{2,1,0:T(8,128)(2,1)S(1)} async-done(((bf16[4,512,256]{2,1,0:T(8,128)(2,1)}), bf16[4,512,256]{2,1,0:T(8,128)(2,1)S(1)}, u32[]{:S(2)}, u32[]{:S(2)}) %all-to-all-start.1) | async-done | bytes 1048608 | tf_op jit(solution)/shard_map/all_to_all | solution.py:382
  85.8 0.6 copy.52
  86.4 3.5 %fusion.21 = f32[2,512,2,2,64]{1,4,3,2,0:T(8,128)S(1)} fusion(bf16[2,512,2048,1,1]{2,1,4,3,0:T(8,128)(2,1)} %bitcast.144, bf16[2,2,64,2048,1]{3,2,1,0,4:T(8,128)(2,1)S(1)} %bitcast.156), kind=kOutput, calls=%fused_computation.76 | convolution fusion | flops 1073741824 | bytes 6291456 | tf_op jit(solution)/shard_map/dot_general | solution.py:385
  90.0 0.8 copy.56
  91.0 0.9 maximum_multiply_fusion.2.t_ref
  91.8 0.8 dynamic-slice_bitcast_fusion.2
  92.6 0.9 dynamic-slice_bitcast_fusion
  93.5 0.3 multiply_subtract_fusion.4
  93.8 1.3 fusion.1.t_ref
  95.1 6.9 %shard_map.364.ys_ref = bf16[1,3,512,1024]{3,2,1,0:T(8,128)(2,1)} custom-call(bf16[1,2,512,512]{3,2,1,0:T(8,128)(2,1)} %all-gather.8.cloned.1.call-done.x_ref, f32[2,512,512]{2,1,0:T(8,128)} %bitcast.167, f32[2,512,512]{2,1,0:T(8,128)} %get-tuple-element.31.gx_ref, f32[2,512,512]{2,1,0:T(8,128)} %get-tuple-element.32.gy_ref, ...), custom_call_target="tpu_custom_call" | custom-call | flops 3221225472 | bytes 12582912 | tf_op jit(solution)/shard_map/pallas_call | solution.py:171
  102.0 1.1 all-gather.12.cloned.1.call-done
  103.1 6.9 %shard_map.368.yp_ref = bf16[1,3,512,1024]{3,2,1,0:T(8,128)(2,1)} custom-call(bf16[1,2,512,512]{3,2,1,0:T(8,128)(2,1)} %bitcast.170, f32[2,512,512]{2,1,0:T(8,128)} %bitcast.168, f32[2,512,512]{2,1,0:T(8,128)} %get-tuple-element.31.gx_ref, f32[2,512,512]{2,1,0:T(8,128)} %get-tuple-element.32.gy_ref, bf16[2,256,512]{2,1,0:T(8,128)(2,1)} %maximum_multiply_fusion.2.t_ref), custom_call_target="tpu_custom_call" | custom-call | flops 3221225472 | bytes 12582912 | tf_op jit(solution)/shard_map/pallas_call | solution.py:171
  110.0 11.4 %all-gather.10.cloned.1.call-done.x_ref = bf16[1,2,512,512]{3,2,1,0:T(8,128)(2,1)} async-done(((bf16[1,2,512,128]{3,2,1,0:T(8,128)(2,1)}), bf16[1,2,512,512]{3,2,1,0:T(8,128)(2,1)}) %all-gather.10.cloned.1.call-update) | async-done | bytes 1048592 | tf_op jit(solution)/shard_map/all_gather | solution.py:392
  121.4 6.9 %shard_map.365.yd_ref = bf16[1,3,512,1024]{3,2,1,0:T(8,128)(2,1)} custom-call(bf16[1,2,512,512]{3,2,1,0:T(8,128)(2,1)} %all-gather.10.cloned.1.call-done.x_ref, f32[2,512,512]{2,1,0:T(8,128)} %bitcast.169, f32[2,512,512]{2,1,0:T(8,128)} %get-tuple-element.31.gx_ref, f32[2,512,512]{2,1,0:T(8,128)} %get-tuple-element.32.gy_ref, ...), custom_call_target="tpu_custom_call" | custom-call | flops 3221225472 | bytes 12582912 | tf_op jit(solution)/shard_map/pallas_call | solution.py:171
  128.3 21.6 %shard_map.366 = (bf16[4,512,512]{2,1,0:T(8,128)(2,1)}, bf16[2,3,512,1024]{3,2,1,0:T(8,128)(2,1)}) custom-call(bf16[1,3,512,1024]{3,2,1,0:T(8,128)(2,1)} %shard_map.364.ys_ref, bf16[1,3,512,1024]{3,2,1,0:T(8,128)(2,1)} %shard_map.365.yd_ref, bf16[2,1024,512]{2,1,0:T(8,128)(2,1)} %pad_maximum_fusion.f_ref), custom_call_target="tpu_custom_call" | custom-call | flops 8589934592 | bytes 12582912 | tf_op jit(solution)/shard_map/pallas_call | solution.py:281
  149.9 6.1 %shard_map.367 = bf16[4,2,512,128]{3,2,1,0:T(8,128)(2,1)} custom-call(bf16[4,512,512]{2,1,0:T(8,128)(2,1)} %get-tuple-element.34.a_ref, bf16[1024,512]{1,0:T(8,128)(2,1)} %fusion.1.t_ref, f32[2,1,512]{2,1,0:T(1,128)} %constant.135.clone.lx_ref, bf16[256,256]{1,0:T(8,128)(2,1)} %constant.137.clone.perm_ref), custom_call_target="tpu_custom_call" | custom-call | flops 2147483648 | bytes 3145728 | tf_op jit(solution)/shard_map/pallas_call | solution.py:122
  156.0 3.6 %all-to-all-start.2 = ((bf16[4,1024,128]{2,1,0:T(8,128)(2,1)}), bf16[4,1024,128]{2,1,0:T(8,128)(2,1)S(1)}, u32[]{:S(2)}, u32[]{:S(2)}) async-start(bf16[4,1024,128]{2,1,0:T(8,128)(2,1)} %bitcast.155), calls=%async_computation.2 | async-start | bytes 2097152 | tf_op jit(solution)/shard_map/all_to_all | solution.py:430
  159.7 0.6 pad.22.tab_ref
  160.3 1.9 shard_map.369
  162.2 14.9 %shard_map.370.a_ref = bf16[4,512,512]{2,1,0:T(8,128)(2,1)} custom-call(bf16[1,3,512,1024]{3,2,1,0:T(8,128)(2,1)} %shard_map.368.yp_ref, bf16[2,3,512,1024]{3,2,1,0:T(8,128)(2,1)} %get-tuple-element.38.own_ref, bf16[2,1024,512]{2,1,0:T(8,128)(2,1)} %pad_maximum_fusion.f_ref), custom_call_target="tpu_custom_call" | custom-call | flops 5368709120 | bytes 12582912 | tf_op jit(solution)/shard_map/pallas_call | solution.py:288
  177.1 6.2 %shard_map.371 = bf16[4,2,512,128]{3,2,1,0:T(8,128)(2,1)} custom-call(bf16[4,512,512]{2,1,0:T(8,128)(2,1)} %shard_map.370.a_ref, bf16[1024,512]{1,0:T(8,128)(2,1)} %fusion.1.t_ref, f32[2,1,512]{2,1,0:T(1,128)} %constant.135.clone.lx_ref, bf16[256,256]{1,0:T(8,128)(2,1)} %constant.137.clone.perm_ref), custom_call_target="tpu_custom_call" | custom-call | flops 2147483648 | bytes 3145728 | tf_op jit(solution)/shard_map/pallas_call | solution.py:122
  183.3 0.1 convert_reduce_fusion.1
  183.5 3.5 %all-to-all-start.3 = ((bf16[4,1024,128]{2,1,0:T(8,128)(2,1)}), bf16[4,1024,128]{2,1,0:T(8,128)(2,1)S(1)}, u32[]{:S(2)}, u32[]{:S(2)}) async-start(bf16[4,1024,128]{2,1,0:T(8,128)(2,1)} %bitcast.54), calls=%async_computation.3 | async-start | bytes 2097152 | tf_op jit(solution)/shard_map/all_to_all | solution.py:430
  187.0 1.5 collective-permute-start.3
  188.6 12.9 %all-to-all-done.3 = bf16[4,1024,128]{2,1,0:T(8,128)(2,1)S(1)} async-done(((bf16[4,1024,128]{2,1,0:T(8,128)(2,1)}), bf16[4,1024,128]{2,1,0:T(8,128)(2,1)S(1)}, u32[]{:S(2)}, u32[]{:S(2)}) %all-to-all-start.3) | async-done | bytes 1048608 | tf_op jit(solution)/shard_map/all_to_all | solution.py:430
  201.5 0.1 convert_reduce_fusion
  201.7 1.5 collective-permute-start.4
  203.2 0.1 add_bitcast_fusion.1
  203.3 6.3 %collective-permute-done.4 = bf16[2,512,128]{2,1,0:T(8,128)(2,1)S(1)} collective-permute-done((bf16[2,512,128]{2,1,0:T(8,128)(2,1)S(1)}, bf16[2,512,128]{2,1,0:T(8,128)(2,1)S(1)}, u32[]{:S(2)}, u32[]{:S(2)}) %collective-permute-start.4) | collective-permute-done | bytes 262176 | tf_op jit(solution)/shard_map/ppermute | solution.py:437
  209.6 0.1 add_bitcast_fusion
  209.7 1.0 maximum_bitcast_fusion
  (68 shorter events, 0.6 us)
Async XLA Ops:
  6.5 2.3 %copy-start.17 = (pred[512]{0:T(512)(128)(4,1)S(1)}, pred[512]{0:T(512)(128)(4,1)}, u32[]{:S(2)}) copy-start(pred[512]{0:T(512)(128)(4,1)} %constant.152) | copy-start | bytes 1540
  10.0 1.5 copy-start.14
  16.8 4.5 %copy-start.1 = (s32[512,128]{1,0:T(8,128)S(1)}, s32[512,128]{1,0:T(8,128)}, u32[]{:S(2)}) copy-start(s32[512,128]{1,0:T(8,128)} %idx_ref.1) | copy-start | bytes 786436
  16.8 4.5 %copy-start.2 = (bf16[512,512]{1,0:T(8,128)(2,1)S(1)}, bf16[512,512]{1,0:T(8,128)(2,1)}, u32[]{:S(2)}) copy-start(bf16[512,512]{1,0:T(8,128)(2,1)} %constant.133.clone) | copy-start | bytes 1572868
  16.8 4.5 %copy-start.9 = (bf16[128,256]{1,0:T(8,128)(2,1)S(1)}, bf16[128,256]{1,0:T(8,128)(2,1)}, u32[]{:S(2)}) copy-start(bf16[128,256]{1,0:T(8,128)(2,1)} %constant.134.clone) | copy-start | bytes 196612
  16.8 6.0 %copy-start.3 = (f32[32,2048]{1,0:T(8,128)S(1)}, f32[32,2048]{1,0:T(8,128)}, u32[]{:S(2)}) copy-start(f32[32,2048]{1,0:T(8,128)} %constant.121.clone) | copy-start | bytes 786436
  16.8 6.0 %copy-start.4 = (f32[32,2048]{1,0:T(8,128)S(1)}, f32[32,2048]{1,0:T(8,128)}, u32[]{:S(2)}) copy-start(f32[32,2048]{1,0:T(8,128)} %constant.122.clone) | copy-start | bytes 786436
  16.8 6.0 %copy-start.5 = (f32[8,2048]{1,0:T(8,128)S(1)}, f32[8,2048]{1,0:T(8,128)}, u32[]{:S(2)}) copy-start(f32[8,2048]{1,0:T(8,128)} %constant.119.clone) | copy-start | bytes 196612
  16.8 6.0 %copy-start.6 = (f32[8,2048]{1,0:T(8,128)S(1)}, f32[8,2048]{1,0:T(8,128)}, u32[]{:S(2)}) copy-start(f32[8,2048]{1,0:T(8,128)} %constant.120.clone) | copy-start | bytes 196612
  16.8 6.0 %copy-start.7 = (f32[8,2048]{1,0:T(8,128)S(1)}, f32[8,2048]{1,0:T(8,128)}, u32[]{:S(2)}) copy-start(f32[8,2048]{1,0:T(8,128)} %constant.123.clone) | copy-start | bytes 196612
  16.8 6.0 %copy-start.8 = (f32[8,2048]{1,0:T(8,128)S(1)}, f32[8,2048]{1,0:T(8,128)}, u32[]{:S(2)}) copy-start(f32[8,2048]{1,0:T(8,128)} %constant.124.clone) | copy-start | bytes 196612
  16.8 35.4 %all-to-all-start = ((bf16[4,512,256]{2,1,0:T(8,128)(2,1)}), bf16[4,512,256]{2,1,0:T(8,128)(2,1)S(1)}, u32[]{:S(2)}, u32[]{:S(2)}) async-start(bf16[4,512,256]{2,1,0:T(8,128)(2,1)} %shard_map.361), calls=%async_computation | async-start | bytes 2097152 | tf_op jit(solution)/shard_map/all_to_all | solution.py:382
  21.2 21.7 %all-gather.6.cloned.1.call-start = ((), (), s32[]{:S(2)}) async-start(), calls=%async_computation.4 | async-start | bytes 1310720 | tf_op jit(solution)/shard_map/all_gather | solution.py:365
  22.7 72.4 %all-gather.8.cloned.1.call-start = ((), (), s32[]{:S(2)}) async-start(), calls=%async_computation.5 | async-start | bytes 1310720 | tf_op jit(solution)/shard_map/all_gather | solution.py:392
  24.0 2.7 %copy-start.15 = (f32[1,64]{1,0:T(1,128)S(1)}, f32[1,64]{1,0:T(1,128)}, u32[]{:S(2)}) copy-start(f32[1,64]{1,0:T(1,128)} %param.43) | copy-start | bytes 772
  24.0 2.7 %copy-start.16 = (f32[1,64]{1,0:T(1,128)S(1)}, f32[1,64]{1,0:T(1,128)}, u32[]{:S(2)}) copy-start(f32[1,64]{1,0:T(1,128)} %param.44) | copy-start | bytes 772
  27.3 21.0 %copy-start.12 = (f32[2,512]{1,0:T(2,128)S(1)}, f32[2,512]{1,0:T(2,128)}, u32[]{:S(2)}) copy-start(f32[2,512]{1,0:T(2,128)} %constant.153) | copy-start | bytes 12292
  27.3 21.0 %copy-start.13 = (f32[512]{0:T(512)S(1)}, f32[512]{0:T(512)}, u32[]{:S(2)}) copy-start(f32[512]{0:T(512)} %constant.154) | copy-start | bytes 6148
  56.6 8.8 %copy-start.10 = (f32[32,512]{1,0:T(8,128)S(1)}, f32[32,512]{1,0:T(8,128)}, u32[]{:S(2)}) copy-start(f32[32,512]{1,0:T(8,128)} %constant.127.clone) | copy-start | bytes 196612
  56.6 8.8 %copy-start.11 = (f32[32,512]{1,0:T(8,128)S(1)}, f32[32,512]{1,0:T(8,128)}, u32[]{:S(2)}) copy-start(f32[32,512]{1,0:T(8,128)} %constant.128.clone) | copy-start | bytes 196612
  57.3 12.0 %copy-start.18 = (s32[4]{0:T(128)S(1)}, s32[4]{0:T(128)}, u32[]{:S(2)}) copy-start(s32[4]{0:T(128)} %param.46) | copy-start | bytes 52
  59.1 12.8 %collective-permute-start = (bf16[2,512,128]{2,1,0:T(8,128)(2,1)S(1)}, bf16[2,512,128]{2,1,0:T(8,128)(2,1)S(1)}, u32[]{:S(2)}, u32[]{:S(2)}) collective-permute-start(bf16[2,512,128]{2,1,0:T(8,128)(2,1)S(1)} %copy.57), channel_id=1, source_target_pairs={{24,0},{0,8},{8,16},{16,24},{25,1},{1,9},{9,17},{17,25},{26,2},{2,... | collective-permute-start | bytes 786440 | tf_op jit(solution)/shard_map/ppermute | solution.py:408
  61.4 20.1 %collective-permute-start.1 = (bf16[2,512,128]{2,1,0:T(8,128)(2,1)S(1)}, bf16[2,512,128]{2,1,0:T(8,128)(2,1)S(1)}, u32[]{:S(2)}, u32[]{:S(2)}) collective-permute-start(bf16[2,512,128]{2,1,0:T(8,128)(2,1)S(1)} %copy.57), channel_id=1, source_target_pairs={{16,0},{24,8},{0,16},{8,24},{17,1},{25,9},{1,17},{9,25},{18,2},{26... | collective-permute-start | bytes 786440 | tf_op jit(solution)/shard_map/ppermute | solution.py:408
  64.0 17.5 %collective-permute-start.2 = (bf16[2,512,128]{2,1,0:T(8,128)(2,1)S(1)}, bf16[2,512,128]{2,1,0:T(8,128)(2,1)S(1)}, u32[]{:S(2)}, u32[]{:S(2)}) collective-permute-start(bf16[2,512,128]{2,1,0:T(8,128)(2,1)S(1)} %copy.57), channel_id=1, source_target_pairs={{8,0},{16,8},{24,16},{0,24},{9,1},{17,9},{25,17},{1,25},{10,2},{18... | collective-permute-start | bytes 786440 | tf_op jit(solution)/shard_map/ppermute | solution.py:408
  65.5 20.3 %all-to-all-start.1 = ((bf16[4,512,256]{2,1,0:T(8,128)(2,1)}), bf16[4,512,256]{2,1,0:T(8,128)(2,1)S(1)}, u32[]{:S(2)}, u32[]{:S(2)}) async-start(bf16[4,512,256]{2,1,0:T(8,128)(2,1)} %shard_map.363), calls=%async_computation.1 | async-start | bytes 2097152 | tf_op jit(solution)/shard_map/all_to_all | solution.py:382
  69.2 33.9 %all-gather.12.cloned.1.call-start = ((), (), s32[]{:S(2)}) async-start(), calls=%async_computation.7 | async-start | bytes 1310720 | tf_op jit(solution)/shard_map/all_gather | solution.py:392
  82.3 39.1 %all-gather.10.cloned.1.call-start = ((), (), s32[]{:S(2)}) async-start(), calls=%async_computation.6 | async-start | bytes 1310720 | tf_op jit(solution)/shard_map/all_gather | solution.py:392
  156.0 3.7 %copy-start.19 = (f32[64]{0:T(128)S(1)}, f32[64]{0:T(128)}, u32[]{:S(2)}) copy-start(f32[64]{0:T(128)} %param.45) | copy-start | bytes 772
  156.0 27.3 %all-to-all-start.2 = ((bf16[4,1024,128]{2,1,0:T(8,128)(2,1)}), bf16[4,1024,128]{2,1,0:T(8,128)(2,1)S(1)}, u32[]{:S(2)}, u32[]{:S(2)}) async-start(bf16[4,1024,128]{2,1,0:T(8,128)(2,1)} %bitcast.155), calls=%async_computation.2 | async-start | bytes 2097152 | tf_op jit(solution)/shard_map/all_to_all | solution.py:430
  177.1 6.3 %copy-start = (f32[512,128]{1,0:T(8,128)S(1)}, f32[512,128]{1,0:T(8,128)}, u32[]{:S(2)}) copy-start(f32[512,128]{1,0:T(8,128)} %shard_map.369) | copy-start | bytes 786436
  183.5 18.0 %all-to-all-start.3 = ((bf16[4,1024,128]{2,1,0:T(8,128)(2,1)}), bf16[4,1024,128]{2,1,0:T(8,128)(2,1)S(1)}, u32[]{:S(2)}, u32[]{:S(2)}) async-start(bf16[4,1024,128]{2,1,0:T(8,128)(2,1)} %bitcast.54), calls=%async_computation.3 | async-start | bytes 2097152 | tf_op jit(solution)/shard_map/all_to_all | solution.py:430
  187.0 16.2 %collective-permute-start.3 = (bf16[2,512,128]{2,1,0:T(8,128)(2,1)S(1)}, bf16[2,512,128]{2,1,0:T(8,128)(2,1)S(1)}, u32[]{:S(2)}, u32[]{:S(2)}) collective-permute-start(bf16[2,512,128]{2,1,0:T(8,128)(2,1)S(1)} %multiply_convert_fusion.1), channel_id=1, source_target_pairs={{0,1},{1,0},{2,3},{3,2},{4,5},{5,4},{6,7},{7,6},{8,9},{9,8},{10,11... | collective-permute-start | bytes 786440 | tf_op jit(solution)/shard_map/ppermute | solution.py:437
  201.7 7.9 %collective-permute-start.4 = (bf16[2,512,128]{2,1,0:T(8,128)(2,1)S(1)}, bf16[2,512,128]{2,1,0:T(8,128)(2,1)S(1)}, u32[]{:S(2)}, u32[]{:S(2)}) collective-permute-start(bf16[2,512,128]{2,1,0:T(8,128)(2,1)S(1)} %multiply_convert_fusion), channel_id=1, source_target_pairs={{0,1},{1,0},{2,3},{3,2},{4,5},{5,4},{6,7},{7,6},{8,9},{9,8},{10,11... | collective-permute-start | bytes 786440 | tf_op jit(solution)/shard_map/ppermute | solution.py:437
Sparse Core Ops, SparseCore 0:
  23.6 19.2 all-gather.5
  58.3 19.9 all-gather.7
  82.4 20.6 all-gather.11
  104.5 16.8 all-gather.9
